TPU v7x, 32 devices: a whole 2x2x4 slice. The times are simulated.
32 devices in a mesh: ctx: 8 (over z, x), fsdp: 4 (over y, core).
Axes of the slice: x: 2, y: 2, z: 4, core: 2. Of those that a mesh axis runs over, the one named last changes fastest.
Arguments:
- hidden_in: bfloat16 [4, 1024, 2048], P('fsdp', 'ctx'), may hold values from -6 to 6
- positions: int32 [4, 1024], P('fsdp'), may hold values from 0 to 1023, as said below
- ln_gain: bfloat16 [2048], P(('ctx', 'fsdp')), may hold values from 0.25 to 1.75
- ln_bias: bfloat16 [2048], P(('ctx', 'fsdp')), may hold values from -1.75 to 1.75
- w_qkv: bfloat16 [6144, 2048], P(('ctx', 'fsdp')), may hold values from -0.125 to 0.125
- b_qkv: bfloat16 [6144], P(('ctx', 'fsdp')), may hold values from -1.75 to 1.75
- w_dense: bfloat16 [2048, 2048], P(('ctx', 'fsdp')), may hold values from -2 to 2
- b_dense: bfloat16 [2048], P(('ctx', 'fsdp')), may hold values from -1.75 to 1.75
- w_fc1: bfloat16 [8192, 2048], P(('ctx', 'fsdp')), may hold values from -0.125 to 0.125
- b_fc1: bfloat16 [8192], P(('ctx', 'fsdp')), may hold values from -1.75 to 1.75
- w_fc2: bfloat16 [2048, 8192], P(('ctx', 'fsdp')), may hold values from -0.09375 to 0.09375
- b_fc2: bfloat16 [2048], P(('ctx', 'fsdp')), may hold values from -1.75 to 1.75
- out_grad: bfloat16 [4, 1024, 2048], P('fsdp', 'ctx'), may hold values from -6 to 6
Outputs:
- hidden_out: bfloat16 [4, 1024, 2048], P('fsdp', 'ctx')
- grad_in: float32 [4, 1024, 2048], P('fsdp', 'ctx')
- grad_ln_gain: float32 [2048], P(('ctx', 'fsdp'))
- grad_ln_bias: float32 [2048], P(('ctx', 'fsdp'))
- grad_w_qkv: float32 [6144, 2048], P(('ctx', 'fsdp'))
- grad_b_qkv: float32 [6144], P(('ctx', 'fsdp'))
- grad_w_dense: float32 [2048, 2048], P(('ctx', 'fsdp'))
- grad_b_dense: float32 [2048], P(('ctx', 'fsdp'))
- grad_w_fc1: float32 [8192, 2048], P(('ctx', 'fsdp'))
- grad_b_fc1: float32 [8192], P(('ctx', 'fsdp'))
- grad_w_fc2: float32 [2048, 8192], P(('ctx', 'fsdp'))
- grad_b_fc2: float32 [2048], P(('ctx', 'fsdp'))
Inputs may be any that keep to these rules, and one draw needn't show every extreme that they name: For each sequence, stored columns 2 b * 64 to 2 b * 64 + 2 * 64 - 1 hold two runs of 64 consecutive rising positions, one starting at j * 64 and one at (15 - j) * 64, in either order; every position of a sequence appears exactly once.
All inputs are finite; a program needn't handle non-finite values.
Results may differ from a plain program's by a relative error of at most 0.012.
Values may be sent and summed in bfloat16 or wider, within the bound.
A program may use at most 512 MiB of HBM per device.

v0:
```python
import jax
import jax.numpy as jnp
from jax import lax
from jax.sharding import PartitionSpec as P

HEAD_DIM = 64
ROT_DIM = 32


EPSILON = 1e-05
SCORE_SCALE = 0.125


def frequencies():
    half_rot = ROT_DIM // 2
    return jnp.power(10000.0, -jnp.arange(half_rot, dtype=jnp.float32) / half_rot)


def rotate(tensor, angles):
    half_rot = ROT_DIM // 2
    cosine = jnp.cos(angles)[:, None, :]
    sine_part = jnp.sin(angles)[:, None, :]
    leading = tensor[..., :half_rot]
    trailing = tensor[..., half_rot:ROT_DIM]
    return jnp.concatenate(
        [
            leading * cosine - trailing * sine_part,
            trailing * cosine + leading * sine_part,
            tensor[..., ROT_DIM:],
        ],
        axis=-1,
    )


def gelu_tanh(values):
    inner_arg = 0.7978845608028654 * (values + 0.044715 * values * values * values)
    return 0.5 * values * (1.0 + jnp.tanh(inner_arg))


def normalize(values, gain_vec, shift_vec):
    centered = values - jnp.mean(values, axis=-1, keepdims=True)
    variance = jnp.mean(centered * centered, axis=-1, keepdims=True)
    return centered * lax.rsqrt(variance + EPSILON) * gain_vec + shift_vec


def column_group(matrix, column_start, group_width, per_group):
    return lax.dynamic_slice_in_dim(matrix, column_start, group_width, 1).reshape(
        matrix.shape[0], per_group, HEAD_DIM
    )


def masked_scores(query_grp, key_grp, allowed):
    raw_scores = (
        jnp.einsum("qhd,khd->hqk", query_grp, key_grp, preferred_element_type=jnp.float32)
        * SCORE_SCALE
    )
    return jnp.where(allowed[None], raw_scores, -1e30)


def body(
    hidden_in,
    positions,
    ln_gain,
    ln_bias,
    w_qkv,
    b_qkv,
    w_dense,
    b_dense,
    w_fc1,
    b_fc1,
    w_fc2,
    b_fc2,
    out_grad,
):
    seq_count, local_len, model_width = hidden_in.shape
    row_count = seq_count * local_len
    heads_total = model_width // HEAD_DIM
    per_group = min(8, heads_total)
    group_width = per_group * HEAD_DIM
    group_count = heads_total // per_group
    head_shape = (row_count, heads_total, HEAD_DIM)
    seq_shape = (seq_count, local_len, model_width)
    inputs_flat = hidden_in.reshape(row_count, model_width).astype(jnp.float32)
    grad_low = out_grad.reshape(row_count, model_width)
    gain_all, shift_all, qkv_all, qkv_bias, up_all, up_bias = (
        lax.all_gather(ln_gain, ("ctx", "fsdp"), axis=0, tiled=True),
        lax.all_gather(ln_bias, ("ctx", "fsdp"), axis=0, tiled=True),
        lax.all_gather(w_qkv, ("ctx", "fsdp"), axis=0, tiled=True),
        lax.all_gather(b_qkv, ("ctx", "fsdp"), axis=0, tiled=True),
        lax.all_gather(w_fc1, ("ctx", "fsdp"), axis=0, tiled=True),
        lax.all_gather(b_fc1, ("ctx", "fsdp"), axis=0, tiled=True),
    )
    gain_wide = gain_all.astype(jnp.float32)
    shift_wide = shift_all.astype(jnp.float32)
    normed, norm_back = jax.vjp(normalize, inputs_flat, gain_wide, shift_wide)
    normed_low = normed.astype(jnp.bfloat16)
    mixed = jnp.einsum(
        "td,od->to", normed_low, qkv_all, preferred_element_type=jnp.float32
    ) + qkv_bias.astype(jnp.float32)
    upward = jnp.einsum(
        "td,fd->tf", normed_low, up_all, preferred_element_type=jnp.float32
    ) + up_bias.astype(jnp.float32)
    gelu_values, gelu_back = jax.vjp(gelu_tanh, upward)
    activated = gelu_values.astype(jnp.bfloat16)
    own_pos = lax.dynamic_slice_in_dim(positions, lax.axis_index("ctx") * local_len, local_len, 1)
    angles = own_pos.reshape(row_count).astype(jnp.float32)[:, None] * frequencies()[None, :]
    queries = (
        rotate(mixed[:, :model_width].reshape(head_shape), angles)
        .reshape(seq_shape)
        .astype(jnp.bfloat16)
    )
    keys_own = (
        rotate(mixed[:, model_width : 2 * model_width].reshape(head_shape), angles)
        .reshape(seq_shape)
        .astype(jnp.bfloat16)
    )
    values_own = mixed[:, 2 * model_width :].reshape(seq_shape).astype(jnp.bfloat16)
    keys_all, values_all = (
        lax.all_gather(keys_own, "ctx", axis=1, tiled=True),
        lax.all_gather(values_own, "ctx", axis=1, tiled=True),
    )
    full_len = keys_all.shape[1]
    sequence = 0
    query_seq = queries[sequence]
    key_seq = keys_all[sequence]
    value_seq = values_all[sequence]
    allowed = positions[sequence][None, :] <= own_pos[sequence][:, None]

    def attend_forward(group_index, state_pair):
        context_acc, lse_acc = state_pair
        column_start = group_index * group_width
        scores = masked_scores(
            column_group(query_seq, column_start, group_width, per_group),
            column_group(key_seq, column_start, group_width, per_group),
            allowed,
        )
        row_peak = jnp.max(scores, axis=-1, keepdims=True)
        exp_scores = jnp.exp(scores - row_peak)
        exp_total = jnp.sum(exp_scores, axis=-1, keepdims=True)
        soft_low = (exp_scores / exp_total).astype(jnp.bfloat16)
        context_grp = jnp.einsum(
            "hqk,khd->qhd",
            soft_low,
            column_group(value_seq, column_start, group_width, per_group),
            preferred_element_type=jnp.float32,
        )
        context_acc = lax.dynamic_update_slice_in_dim(
            context_acc, context_grp.reshape(local_len, group_width), column_start, 1
        )
        lse_acc = lax.dynamic_update_slice_in_dim(
            lse_acc, (row_peak + jnp.log(exp_total))[:, :, 0], group_index * per_group, 0
        )
        return (context_acc, lse_acc)

    start_state = (
        jnp.zeros((local_len, model_width), jnp.float32),
        jnp.zeros((heads_total, local_len), jnp.float32),
    )
    context_seq, lse_seq = lax.fori_loop(0, group_count, attend_forward, start_state)
    lse_rows = [lse_seq]
    context_low = context_seq.astype(jnp.bfloat16)
    dense_rows = lax.all_gather(w_dense, ("ctx", "fsdp"), axis=0, tiled=True)
    dense_piece = lax.all_gather(b_dense, ("ctx", "fsdp"), axis=0, tiled=True)
    down_rows = lax.all_gather(w_fc2, ("ctx", "fsdp"), axis=0, tiled=True)
    down_piece = lax.all_gather(b_fc2, ("ctx", "fsdp"), axis=0, tiled=True)
    part_cols = (
        jnp.einsum("ti,oi->to", context_low, dense_rows, preferred_element_type=jnp.float32)
        + dense_piece.astype(jnp.float32)
        + jnp.einsum("tf,of->to", activated, down_rows, preferred_element_type=jnp.float32)
        + down_piece.astype(jnp.float32)
    )
    total = inputs_flat + part_cols
    hidden_out = total.astype(jnp.bfloat16).reshape(seq_shape)
    dense_rows = lax.all_gather(w_dense, ("ctx", "fsdp"), axis=0, tiled=True)
    down_rows = lax.all_gather(w_fc2, ("ctx", "fsdp"), axis=0, tiled=True)
    grad_context = jnp.einsum("to,oi->ti", grad_low, dense_rows, preferred_element_type=jnp.float32)
    grad_activated = jnp.einsum(
        "to,of->tf", grad_low, down_rows, preferred_element_type=jnp.float32
    )
    dense_term = jnp.einsum("to,ti->oi", grad_low, context_low, preferred_element_type=jnp.float32)
    down_term = jnp.einsum("to,tf->of", grad_low, activated, preferred_element_type=jnp.float32)
    bias_out_term = jnp.sum(grad_low, axis=0, dtype=jnp.float32)
    grad_dense, grad_bias_out, grad_down = (
        lax.psum_scatter(dense_term, ("ctx", "fsdp"), scatter_dimension=0, tiled=True),
        lax.psum_scatter(bias_out_term, ("ctx", "fsdp"), scatter_dimension=0, tiled=True),
        lax.psum_scatter(down_term, ("ctx", "fsdp"), scatter_dimension=0, tiled=True),
    )
    grad_upward = gelu_back(grad_activated)[0].astype(jnp.bfloat16)
    context_grad = grad_context.astype(jnp.bfloat16).reshape(seq_shape)
    sequence = 0
    query_seq = queries[sequence]
    key_seq = keys_all[sequence]
    value_seq = values_all[sequence]
    grad_seq = context_grad[sequence]
    lse_seq = lse_rows[sequence]
    allowed = positions[sequence][None, :] <= own_pos[sequence][:, None]

    def attend_back(group_index, state_triple):
        query_acc, key_acc, value_acc = state_triple
        column_start = group_index * group_width
        query_grp = column_group(query_seq, column_start, group_width, per_group)
        key_grp = column_group(key_seq, column_start, group_width, per_group)
        value_grp = column_group(value_seq, column_start, group_width, per_group)
        grad_grp = column_group(grad_seq, column_start, group_width, per_group)
        lse_grp = lax.dynamic_slice_in_dim(lse_seq, group_index * per_group, per_group, 0)
        soft_probs = jnp.exp(masked_scores(query_grp, key_grp, allowed) - lse_grp[:, :, None])
        grad_probs = jnp.einsum(
            "qhd,khd->hqk", grad_grp, value_grp, preferred_element_type=jnp.float32
        )
        inner_sum = jnp.sum(soft_probs * grad_probs, axis=-1, keepdims=True)
        grad_scores = (soft_probs * (grad_probs - inner_sum)).astype(jnp.bfloat16)
        grad_query = (
            jnp.einsum("hqk,khd->qhd", grad_scores, key_grp, preferred_element_type=jnp.float32)
            * SCORE_SCALE
        )
        grad_key = (
            jnp.einsum("hqk,qhd->khd", grad_scores, query_grp, preferred_element_type=jnp.float32)
            * SCORE_SCALE
        )
        grad_value = jnp.einsum(
            "hqk,qhd->khd",
            soft_probs.astype(jnp.bfloat16),
            grad_grp,
            preferred_element_type=jnp.float32,
        )
        query_acc = lax.dynamic_update_slice_in_dim(
            query_acc, grad_query.reshape(local_len, group_width), column_start, 1
        )
        key_acc = lax.dynamic_update_slice_in_dim(
            key_acc, grad_key.reshape(full_len, group_width), column_start, 1
        )
        value_acc = lax.dynamic_update_slice_in_dim(
            value_acc, grad_value.reshape(full_len, group_width), column_start, 1
        )
        return (query_acc, key_acc, value_acc)

    start_triple = (
        jnp.zeros((local_len, model_width), jnp.float32),
        jnp.zeros((full_len, model_width), jnp.float32),
        jnp.zeros((full_len, model_width), jnp.float32),
    )
    query_grad_seq, key_grad_seq, value_grad_seq = lax.fori_loop(
        0, group_count, attend_back, start_triple
    )
    key_share = lax.psum_scatter(
        key_grad_seq.astype(jnp.bfloat16), "ctx", scatter_dimension=0, tiled=True
    ).astype(jnp.float32)
    value_share = lax.psum_scatter(
        value_grad_seq.astype(jnp.bfloat16), "ctx", scatter_dimension=0, tiled=True
    ).astype(jnp.float32)
    grad_mixed = jnp.concatenate(
        [
            rotate(query_grad_seq.reshape(head_shape), -angles).reshape(row_count, model_width),
            rotate(key_share.reshape(head_shape), -angles).reshape(row_count, model_width),
            value_share,
        ],
        axis=1,
    ).astype(jnp.bfloat16)
    qkv_back, up_back = (
        lax.all_gather(w_qkv, ("ctx", "fsdp"), axis=0, tiled=True),
        lax.all_gather(w_fc1, ("ctx", "fsdp"), axis=0, tiled=True),
    )
    grad_normed = jnp.einsum(
        "to,od->td", grad_mixed, qkv_back, preferred_element_type=jnp.float32
    ) + jnp.einsum("tf,fd->td", grad_upward, up_back, preferred_element_type=jnp.float32)
    grad_inputs, gain_term, shift_term = norm_back(grad_normed)
    grad_in = (grad_inputs + grad_low.astype(jnp.float32)).reshape(seq_shape)
    qkv_term = jnp.einsum("to,td->od", grad_mixed, normed_low, preferred_element_type=jnp.float32)
    qkv_bias_term = jnp.sum(grad_mixed, axis=0, dtype=jnp.float32)
    up_term = jnp.einsum("tf,td->fd", grad_upward, normed_low, preferred_element_type=jnp.float32)
    up_bias_term = jnp.sum(grad_upward, axis=0, dtype=jnp.float32)
    grad_gain, grad_shift, grad_qkv, grad_qkv_bias, grad_up, grad_up_bias = (
        lax.psum_scatter(gain_term, ("ctx", "fsdp"), scatter_dimension=0, tiled=True),
        lax.psum_scatter(shift_term, ("ctx", "fsdp"), scatter_dimension=0, tiled=True),
        lax.psum_scatter(qkv_term, ("ctx", "fsdp"), scatter_dimension=0, tiled=True),
        lax.psum_scatter(qkv_bias_term, ("ctx", "fsdp"), scatter_dimension=0, tiled=True),
        lax.psum_scatter(up_term, ("ctx", "fsdp"), scatter_dimension=0, tiled=True),
        lax.psum_scatter(up_bias_term, ("ctx", "fsdp"), scatter_dimension=0, tiled=True),
    )
    return (
        hidden_out,
        grad_in,
        grad_gain,
        grad_shift,
        grad_qkv,
        grad_qkv_bias,
        grad_dense,
        grad_bias_out,
        grad_up,
        grad_up_bias,
        grad_down,
        grad_bias_out,
    )


def solution(mesh):
    return jax.shard_map(
        body,
        mesh=mesh,
        in_specs=(
            P("fsdp", "ctx", None),
            P("fsdp", None),
            P(("ctx", "fsdp")),
            P(("ctx", "fsdp")),
            P(("ctx", "fsdp"), None),
            P(("ctx", "fsdp")),
            P(("ctx", "fsdp"), None),
            P(("ctx", "fsdp")),
            P(("ctx", "fsdp"), None),
            P(("ctx", "fsdp")),
            P(("ctx", "fsdp"), None),
            P(("ctx", "fsdp")),
            P("fsdp", "ctx", None),
        ),
        out_specs=(
            P("fsdp", "ctx", None),
            P("fsdp", "ctx", None),
            P(("ctx", "fsdp")),
            P(("ctx", "fsdp")),
            P(("ctx", "fsdp"), None),
            P(("ctx", "fsdp")),
            P(("ctx", "fsdp"), None),
            P(("ctx", "fsdp")),
            P(("ctx", "fsdp"), None),
            P(("ctx", "fsdp")),
            P(("ctx", "fsdp"), None),
            P(("ctx", "fsdp")),
        ),
        check_vma=False,
    )
```

profile of v0, /device:TPU:10, one launch (start us, length us, event | category | flops | bytes accessed | tf_op | source)
XLA Modules:
  0.0 3267.7 jit_solution(599649486222805410)
XLA Ops:
  13.0 43.3 %all-reduce.11 = (bf16[2048]{0:T(1024)(128)(2,1)}, bf16[6144]{0:T(1024)(128)(2,1)S(1)}, bf16[2048]{0:T(1024)(128)(2,1)S(1)}, bf16[2048]{0:T(1024)(128)(2,1)S(1)}, bf16[2048]{0:T(1024)(128)(2,1)}) all-reduce(bf16[2048]{0:T(1024)(128)(2,1)S(1)} %dynamic-update-slice.3, ...), channel_id=1, replica_groups=mesh['ctx'=8,'fsdp'=4] {'ctx','fsdp'}, use_global_device_ids=true, to_apply=%add.3 | all-reduce | flops 14336 | bytes 57344
  59.4 107.1 %all-gather.9.cloned.1.call-done = bf16[6144,2048]{1,0:T(8,128)(2,1)} async-done(((bf16[192,2048]{1,0:T(8,128)(2,1)}), bf16[6144,2048]{1,0:T(8,128)(2,1)}) %all-gather.9.cloned.1.call-update) | async-done | bytes 25165840 | tf_op jit(solution)/shard_map/all_gather | solution.py:88
  166.5 13.3 convolution_add_fusion.1
  187.0 59.9 %all-gather.13.cloned.1.call-done = bf16[2048,2048]{1,0:T(8,128)(2,1)} async-done(((bf16[64,2048]{1,0:T(8,128)(2,1)}), bf16[2048,2048]{1,0:T(8,128)(2,1)}) %all-gather.13.cloned.1.call-update) | async-done | bytes 8388624 | tf_op jit(solution)/shard_map/all_gather | solution.py:162
  247.0 5.4 convolution_convert_fusion
  252.5 67.6 %all-gather.19.cloned.1.call-done = bf16[1024,2048]{1,0:T(8,128)(2,1)} async-done(((bf16[128,2048]{1,0:T(8,128)(2,1)}), bf16[1024,2048]{1,0:T(8,128)(2,1)}) %all-gather.19.cloned.1.call-update) | async-done | bytes 4194320 | tf_op jit(solution)/shard_map/all_gather | solution.py:120
  320.1 6.5 copy.43
  326.6 68.0 %all-gather.11.cloned.1.call-done = bf16[1,1024,2048]{1,2,0:T(8,128)(2,1)} async-done(((bf16[1,128,2048]{1,2,0:T(8,128)(2,1)}), bf16[1,1024,2048]{1,2,0:T(8,128)(2,1)}) %all-gather.11.cloned.1.call-update) | async-done | bytes 4194320 | tf_op jit(solution)/shard_map/all_gather | solution.py:119
  394.6 21.7 while.34
  394.6 1.7 constant_dynamic-slice_fusion.15
  400.1 1.7 constant_dynamic-slice_fusion.15
  405.5 1.7 constant_dynamic-slice_fusion.15
  410.9 1.7 constant_dynamic-slice_fusion.15
  416.5 2.5 broadcast.178
  419.0 2.5 broadcast.178.clone
  421.5 64.6 %while.35 = (s32[]{:T(128)}, f32[128,2048]{0,1:T(8,128)S(1)}, bf16[1024,2048]{0,1:T(8,128)(2,1)}, bf16[1024,2048]{0,1:T(8,128)(2,1)}, bf16[1024,2048]{0,1:T(8,12...) while((s32[]{:T(128)}, f32[128,2048]{0,1:T(8,128)S(1)}, ...), condition=%wide.region_8.9_spmd.clone, body=%wide.region_6.0_spmd.clone.sunk | while | flops 688061440 | bytes 64521016 | solution.py:242
  422.8 2.7 fusion.127
  428.0 4.1 multiply_reduce_fusion.2
  439.0 2.7 fusion.127
  444.2 4.1 multiply_reduce_fusion.2
  455.2 2.7 fusion.127
  460.4 4.1 multiply_reduce_fusion.2
  471.3 2.7 fusion.127
  476.5 4.1 multiply_reduce_fusion.2
  486.1 6.5 copy.48
  492.6 6.6 copy.50
  500.8 34.1 %all-gather.1 = bf16[32,1,256]{2,1,0:T(2,128)(2,1)S(1)} all-gather(bf16[1,1,256]{2,1,0:T(2,128)(2,1)S(1)} %reshape.335), channel_id=1, replica_groups=mesh['ctx'=8,'fsdp'=4] {'ctx','fsdp'}, dimensions={0}, use_global_device_ids=true | all-gather | bytes 16896 | tf_op jit(solution)/shard_map/all_gather | solution.py:91
  535.0 47.1 %reduce-scatter.19.cloned.1.call-done = bf16[128,2048]{1,0:T(8,128)(2,1)} async-done(((bf16[1024,2048]{1,0:T(8,128)(2,1)}), bf16[128,2048]{1,0:T(8,128)(2,1)}) %reduce-scatter.19.cloned.1.call-update) | async-done | bytes 524304
  584.3 89.4 %reduce-scatter.21.cloned.1.call-done = bf16[128,2048]{1,0:T(8,128)(2,1)} async-done(((bf16[1024,2048]{1,0:T(8,128)(2,1)}), bf16[128,2048]{1,0:T(8,128)(2,1)}) %reduce-scatter.21.cloned.1.call-update) | async-done | bytes 524304
  677.5 13.3 fusion.56
  690.8 178.2 %all-gather.15.cloned.1.call-done = bf16[8192,2048]{1,0:T(8,128)(2,1)} async-done(((bf16[256,2048]{1,0:T(8,128)(2,1)}), bf16[8192,2048]{1,0:T(8,128)(2,1)}) %all-gather.15.cloned.1.call-update) | async-done | bytes 33554448 | tf_op jit(solution)/shard_map/all_gather | solution.py:90
  869.1 18.5 convolution_add_fusion
  887.6 177.3 %all-gather.17.cloned.1.call-done = bf16[2048,8192]{1,0:T(8,128)(2,1)} async-done(((bf16[64,8192]{1,0:T(8,128)(2,1)}), bf16[2048,8192]{1,0:T(8,128)(2,1)}) %all-gather.17.cloned.1.call-update) | async-done | bytes 33554448 | tf_op jit(solution)/shard_map/all_gather | solution.py:164
  1064.9 16.8 convert_reduce_fusion
  1081.7 13.7 fusion.65
  1096.4 2.1 convert_reduce_fusion.2
  1098.8 9.1 convolution_bitcast_fusion.1
  1107.9 17.7 copy.52
  1125.6 20.9 fusion.55
  1146.6 23.3 fusion.60
  1170.2 25.4 convolution_bitcast_fusion
  1195.6 61.4 %copy.54 = f32[2048,8192]{1,0:T(8,128)} copy(f32[2048,8192]{0,1:T(8,128)} %convolution_bitcast_fusion) | data formatting | bytes 134217728
  1258.0 6.4 convolution_add_fusion.4
  1264.4 18.0 fusion.29
  1288.3 118.3 %reduce-scatter.23.cloned.1.call-done = f32[64,2048]{1,0:T(8,128)} async-done(((f32[2048,2048]{1,0:T(8,128)}), f32[64,2048]{1,0:T(8,128)}) %reduce-scatter.23.cloned.1.call-update) | async-done | bytes 524304
  1406.7 440.4 %reduce-scatter.15.cloned.1.call-done = f32[192,2048]{1,0:T(8,128)} async-done(((f32[6144,2048]{1,0:T(8,128)}), f32[192,2048]{1,0:T(8,128)}) %reduce-scatter.15.cloned.1.call-update) | async-done | bytes 1572880 | tf_op jit(solution)/shard_map/reduce_scatter | solution.py:275
  1847.0 704.6 %reduce-scatter.17.cloned.1.call-done = f32[256,2048]{1,0:T(8,128)} async-done(((f32[8192,2048]{1,0:T(8,128)}), f32[256,2048]{1,0:T(8,128)}) %reduce-scatter.17.cloned.1.call-update) | async-done | bytes 2097168 | tf_op jit(solution)/shard_map/reduce_scatter | solution.py:277
  2551.6 708.8 %reduce-scatter.25.cloned.1.call-done = f32[64,8192]{1,0:T(8,128)} async-done(((f32[2048,8192]{1,0:T(8,128)}), f32[64,8192]{1,0:T(8,128)}) %reduce-scatter.25.cloned.1.call-update) | async-done | bytes 2097168
  (216 shorter events, 84.4 us)
Async XLA Ops:
  7.2 159.3 %all-gather.9.cloned.1.call-start = ((), (), s32[]{:S(2)}) async-start(), calls=%async_computation.6 | async-start | bytes 25952256 | tf_op jit(solution)/shard_map/all_gather | solution.py:88
  7.9 239.0 %all-gather.13.cloned.1.call-start = ((), (), s32[]{:S(2)}) async-start(), calls=%async_computation.8 | async-start | bytes 8650752 | tf_op jit(solution)/shard_map/all_gather | solution.py:162
  8.7 311.5 %all-gather.19.cloned.1.call-start = ((), (), s32[]{:S(2)}) async-start(), calls=%async_computation.13 | async-start | bytes 4718592 | tf_op jit(solution)/shard_map/all_gather | solution.py:120
  56.3 123.6 %copy-start.12 = (f32[2048]{0:T(1024)}, f32[2048]{0:T(1024)S(1)}, u32[]{:S(2)}) copy-start(f32[2048]{0:T(1024)S(1)} %convert_element_type.115) | copy-start | bytes 24580
  56.3 123.6 %copy-start.10 = (f32[2048]{0:T(1024)}, f32[2048]{0:T(1024)S(1)}, u32[]{:S(2)}) copy-start(f32[2048]{0:T(1024)S(1)} %convert_element_type.114) | copy-start | bytes 24580
  57.5 122.4 %copy-start.15 = (f32[128]{0:T(128)}, f32[128]{0:T(128)S(1)}, u32[]{:S(2)}) copy-start(f32[128]{0:T(128)S(1)} %broadcast_multiply_fusion) | copy-start | bytes 1540
  58.8 0.5 copy-start.21
  59.3 120.5 %copy-start.17 = (f32[128]{0:T(128)}, f32[128]{0:T(128)S(1)}, u32[]{:S(2)}) copy-start(f32[128]{0:T(128)S(1)} %fusion.54) | copy-start | bytes 1540
  59.3 121.5 %copy-start.14 = (s32[1,1024]{1,0:T(1,128)S(1)}, s32[1,1024]{1,0:T(1,128)}, u32[]{:S(2)}) copy-start(s32[1,1024]{1,0:T(1,128)} %param.18) | copy-start | bytes 12292
  180.7 213.9 %all-gather.11.cloned.1.call-start = ((), (), s32[]{:S(2)}) async-start(), calls=%async_computation.7 | async-start | bytes 4718592 | tf_op jit(solution)/shard_map/all_gather | solution.py:119
  182.4 64.5 %copy-start.2 = (bf16[1,128,2048]{2,1,0:T(8,128)(2,1)S(1)}, bf16[1,128,2048]{2,1,0:T(8,128)(2,1)}, u32[]{:S(2)}) copy-start(bf16[1,128,2048]{2,1,0:T(8,128)(2,1)} %param.29) | copy-start | bytes 1572868
  186.7 395.4 %reduce-scatter.19.cloned.1.call-start = ((), (), s32[]{:S(2)}) async-start(), calls=%async_computation.14 | async-start | bytes 4718592
  416.4 5.1 copy-start.7
  428.0 4.1 copy-start
  444.2 4.1 copy-start
  460.4 4.1 copy-start
  476.5 4.1 copy-start
  492.6 181.1 %reduce-scatter.21.cloned.1.call-start = ((), (), s32[]{:S(2)}) async-start(), calls=%async_computation.15 | async-start | bytes 4718592
  499.2 1.6 copy-start.23
  499.3 369.8 %all-gather.15.cloned.1.call-start = ((), (), s32[]{:S(2)}) async-start(), calls=%async_computation.9 | async-start | bytes 34603008 | tf_op jit(solution)/shard_map/all_gather | solution.py:90
  500.0 564.9 %all-gather.17.cloned.1.call-start = ((), (), s32[]{:S(2)}) async-start(), calls=%async_computation.10 | async-start | bytes 34603008 | tf_op jit(solution)/shard_map/all_gather | solution.py:164
  500.8 781.6 %all-reduce.14.cloned.1.call-start = ((), (), s32[]{:S(2)}) async-start(), calls=%async_computation.18 | async-start | bytes 163840
  675.0 15.8 copy-start.4
  676.3 1.1 copy-start.5
  676.3 1.1 copy-start.6
  677.4 191.6 %copy-start.1 = (bf16[1,128,2048]{2,1,0:T(8,128)(2,1)S(1)}, bf16[1,128,2048]{2,1,0:T(8,128)(2,1)}, u32[]{:S(2)}) copy-start(bf16[1,128,2048]{2,1,0:T(8,128)(2,1)} %param.17) | copy-start | bytes 1572868
  677.4 191.6 %copy-start.11 = (f32[2048]{0:T(1024)S(1)}, f32[2048]{0:T(1024)}, u32[]{:S(2)}) copy-start(f32[2048]{0:T(1024)} %copy-done.10) | copy-start | bytes 24580
  677.4 191.6 %copy-start.13 = (f32[2048]{0:T(1024)S(1)}, f32[2048]{0:T(1024)}, u32[]{:S(2)}) copy-start(f32[2048]{0:T(1024)} %copy-done.12) | copy-start | bytes 24580
  677.4 191.6 %copy-start.16 = (f32[128]{0:T(128)S(1)}, f32[128]{0:T(128)}, u32[]{:S(2)}) copy-start(f32[128]{0:T(128)} %copy-done.15) | copy-start | bytes 1540
  677.4 191.6 %copy-start.18 = (f32[128]{0:T(128)S(1)}, f32[128]{0:T(128)}, u32[]{:S(2)}) copy-start(f32[128]{0:T(128)} %copy-done.17) | copy-start | bytes 1540
  869.1 195.8 %copy-start.3 = (bf16[1,128,2048]{2,1,0:T(8,128)(2,1)S(1)}, bf16[1,128,2048]{2,1,0:T(8,128)(2,1)}, u32[]{:S(2)}) copy-start(bf16[1,128,2048]{2,1,0:T(8,128)(2,1)} %param.29) | copy-start | bytes 1572868
  1064.9 16.8 copy-start.9
  1081.7 13.7 copy-start.22
  1098.6 308.1 %reduce-scatter.23.cloned.1.call-start = ((), (), s32[]{:S(2)}) async-start(), calls=%async_computation.16 | async-start | bytes 17301504
  1125.6 721.5 %reduce-scatter.15.cloned.1.call-start = ((), (), s32[]{:S(2)}) async-start(), calls=%async_computation.11 | async-start | bytes 51904512 | tf_op jit(solution)/shard_map/reduce_scatter | solution.py:275
  1146.6 1405.0 %reduce-scatter.17.cloned.1.call-start = ((), (), s32[]{:S(2)}) async-start(), calls=%async_computation.12 | async-start | bytes 69206016 | tf_op jit(solution)/shard_map/reduce_scatter | solution.py:277
  1170.0 2090.4 %reduce-scatter.25.cloned.1.call-start = ((), (), s32[]{:S(2)}) async-start(), calls=%async_computation.17 | async-start | bytes 69206016
  1257.0 0.7 copy-start.20
  1257.0 0.7 copy-start.19
  1257.0 1.0 copy-start.8
  1285.7 1975.3 %copy-start.24 = (f32[64]{0:T(128)}, f32[64]{0:T(128)S(1)}, u32[]{:S(2)}) copy-start(f32[64]{0:T(128)S(1)} %dynamic-slice.3) | copy-start | bytes 772
Sparse Core Ops, SparseCore 0:
  10.9 155.5 all-gather.8
  169.3 77.5 all-gather.12
  249.7 70.4 all-gather.18
  322.6 71.9 all-gather.10
  492.7 89.3 reduce-scatter.18
  586.0 87.6 reduce-scatter.20
  676.6 192.4 all-gather.14
  871.9 192.9 all-gather.16
  1098.7 124.6 all-reduce.13
  1226.1 180.4 reduce-scatter.22
  1413.7 433.3 reduce-scatter.14
  1849.8 701.7 reduce-scatter.16
  2554.5 705.8 reduce-scatter.24
where the time goes:
time: 3280 us; the launch traced here: 3270 us
  waiting for transfers between devices  2770 us (84%)
  matrix products  231 us (7%)
  local copies, waits for them, and re-layouts  153 us (5%)
  blocking collectives  77.4 us (2%)
    unnamed x18, waiting for transfers between devices  967 us
    reduce_scatter x1, waiting for transfers between devices, body(): lax.psum_scatter(up_term, ('ctx', 'fsdp'), scatter_dimension=0, tiled=True)  705 us
    reduce_scatter x1, waiting for transfers between devices, body(): lax.psum_scatter(qkv_term, ('ctx', 'fsdp'), scatter_dimension=0, tiled=True)  440 us
    all_gather x1, waiting for transfers between devices, body(): lax.all_gather(w_fc1, ('ctx', 'fsdp'), axis=0, tiled=True)  178 us
    all_gather x1, waiting for transfers between devices, body(): down_rows = lax.all_gather(w_fc2, ('ctx', 'fsdp'), axis=0, tiled=True)  177 us
    unnamed x72, local copies, waits for them, and re-layouts  114 us
    all_gather x1, waiting for transfers between devices, body(): lax.all_gather(w_qkv, ('ctx', 'fsdp'), axis=0, tiled=True)  107 us
    all_gather x1, waiting for transfers between devices, body(): lax.all_gather(keys_own, 'ctx', axis=1, tiled=True)  68 us
  transfers between devices with their start and end apart: 13, of which 12 were waited for; matrix products, arithmetic and copies ran while one was open for 8% of the time, Pallas kernels for 0%

commit v1 on v0

v1 whole, which is shorter than its diff:
```python
import functools

import jax
import jax.numpy as jnp
from jax import lax
from jax.experimental import pallas as pl
from jax.experimental.pallas import tpu as pltpu
from jax.sharding import PartitionSpec as P

HEAD_DIM = 64
ROT_DIM = 32
RUN = 64
EPSILON = 1e-05
SCORE_SCALE = 0.125
BOTH = ("ctx", "fsdp")
F32 = jnp.float32
LOW = jnp.bfloat16
MESH = pl.DeviceIdType.MESH
SEMAPHORES = 512
VMEM_BYTES = 60 * 1024 * 1024


def gelu_tanh(values):
    inner_arg = 0.7978845608028654 * (values + 0.044715 * values * values * values)
    return 0.5 * values * (1.0 + jnp.tanh(inner_arg))


def gelu_slope(values):
    inner_arg = 0.7978845608028654 * (values + 0.044715 * values * values * values)
    bend = jnp.tanh(inner_arg)
    inner_slope = 0.7978845608028654 * (1.0 + 3.0 * 0.044715 * values * values)
    return 0.5 * (1.0 + bend) + 0.5 * values * (1.0 - bend * bend) * inner_slope


def dot_nt(a, b):
    return lax.dot_general(a, b, (((1,), (1,)), ((), ())), preferred_element_type=F32)


def dot_nn(a, b):
    return lax.dot_general(a, b, (((1,), (0,)), ((), ())), preferred_element_type=F32)


def dot_tn(a, b):
    return lax.dot_general(a, b, (((0,), (0,)), ((), ())), preferred_element_type=F32)


def rope_tables(length):
    half_rot = ROT_DIM // 2
    freqs = jnp.power(10000.0, -jnp.arange(half_rot, dtype=F32) / half_rot)
    angles = jnp.arange(length, dtype=F32)[:, None] * freqs[None, :]
    cosine, sine = jnp.cos(angles), jnp.sin(angles)
    rest = HEAD_DIM - ROT_DIM
    ones, zeros = jnp.ones((length, rest), F32), jnp.zeros((length, rest), F32)
    gap = jnp.zeros((length, half_rot), F32)
    straight = jnp.concatenate([cosine, cosine, ones] * 2, axis=1)
    from_above = jnp.concatenate([-sine, gap, zeros] * 2, axis=1)
    from_below = jnp.concatenate([gap, sine, zeros] * 2, axis=1)
    return straight, from_above, from_below


def attention_kernel(
    order_ref, q_ref, k_ref, v_ref, g_ref, cos_ref, up_ref, down_ref,
    ctx_out, dq_out, dk_out, dv_out,
    q_s, k_s, v_s, g_s, dk_s, dv_s, ctx_s, dq_s,
):
    length, width = q_ref.shape
    half_rot = ROT_DIM // 2
    runs = length // RUN

    def sort_in(i, carry):
        stored = pl.ds(pl.multiple_of(order_ref[i] * RUN, RUN), RUN)
        rows = pl.ds(pl.multiple_of(i * RUN, RUN), RUN)
        cosine, above, below = cos_ref[rows, :], up_ref[rows, :], down_ref[rows, :]

        def turn(u):
            return (
                u * cosine
                + pltpu.roll(u, width - half_rot, 1) * above
                + pltpu.roll(u, half_rot, 1) * below
            )

        q_s[rows, :] = (turn(q_ref[stored, :]).astype(LOW) * SCORE_SCALE).astype(LOW)
        k_s[rows, :] = turn(k_ref[stored, :]).astype(LOW)
        v_s[rows, :] = v_ref[stored, :].astype(LOW)
        g_s[rows, :] = g_ref[stored, :]
        return carry

    lax.fori_loop(0, runs, sort_in, 0)
    dk_s[...] = jnp.zeros_like(dk_s)
    dv_s[...] = jnp.zeros_like(dv_s)

    tile = min(256, length)
    lanes = lax.broadcasted_iota(jnp.int32, (tile, width), 1)
    diagonal = lax.broadcasted_iota(jnp.int32, (tile, tile), 1) <= lax.broadcasted_iota(
        jnp.int32, (tile, tile), 0
    )
    for step in range(length // tile):
        rows = slice(step * tile, (step + 1) * tile)
        reach = (step + 1) * tile
        q_pair, g_pair = q_s[rows, :], g_s[rows, :]
        context = jnp.zeros((tile, width), F32)
        grad_q = jnp.zeros((tile, width), F32)
        for head in range(width // HEAD_DIM):
            mine = (lanes // HEAD_DIM) == head
            q_own = jnp.where(mine, q_pair, jnp.zeros_like(q_pair))
            g_own = jnp.where(mine, g_pair, jnp.zeros_like(g_pair))
            scores = dot_nt(q_own, k_s[:reach, :])
            last = jnp.where(diagonal, scores[:, reach - tile :], -1e30)
            if step > 0:
                scores = jnp.concatenate([scores[:, : reach - tile], last], axis=1)
            else:
                scores = last
            peak = jnp.max(scores, axis=1, keepdims=True)
            exps = jnp.exp(scores - peak)
            probs = exps * (1.0 / jnp.sum(exps, axis=1, keepdims=True))
            probs_low = probs.astype(LOW)
            context = jnp.where(mine, dot_nn(probs_low, v_s[:reach, :]), context)
            grad_probs = dot_nt(g_own, v_s[:reach, :])
            inner = jnp.sum(probs * grad_probs, axis=1, keepdims=True)
            grad_scores = (probs * (grad_probs - inner)).astype(LOW)
            grad_q = jnp.where(mine, dot_nn(grad_scores, k_s[:reach, :]), grad_q)
            dk_s[:reach, :] += dot_tn(grad_scores, q_own)
            dv_s[:reach, :] += dot_tn(probs_low, g_own)
        ctx_s[rows, :] = context.astype(LOW)
        dq_s[rows, :] = grad_q * SCORE_SCALE

    def sort_out(i, carry):
        stored = pl.ds(pl.multiple_of(order_ref[i] * RUN, RUN), RUN)
        rows = pl.ds(pl.multiple_of(i * RUN, RUN), RUN)
        cosine, above, below = cos_ref[rows, :], up_ref[rows, :], down_ref[rows, :]

        def turn_back(u):
            return (
                u * cosine
                - pltpu.roll(u, width - half_rot, 1) * above
                - pltpu.roll(u, half_rot, 1) * below
            )

        ctx_out[stored, :] = ctx_s[rows, :]
        dq_out[stored, :] = turn_back(dq_s[rows, :]).astype(LOW)
        dk_out[stored, :] = turn_back(dk_s[rows, :]).astype(LOW)
        dv_out[stored, :] = dv_s[rows, :].astype(LOW)
        return carry

    lax.fori_loop(0, runs, sort_out, 0)


def attention(order, mixed, grad_context):
    length, width = grad_context.shape
    pair = 2 * HEAD_DIM
    pairs = width // pair
    tables = rope_tables(length)

    def part(offset):
        return pl.BlockSpec((length, pair), lambda i, order_ref: (0, offset * pairs + i))

    whole = pl.BlockSpec((length, pair), lambda i, order_ref: (0, 0))
    half_pairs = length * length * 5 // 8
    result = jax.ShapeDtypeStruct((length, width), LOW)
    return pl.pallas_call(
        attention_kernel,
        grid_spec=pltpu.PrefetchScalarGridSpec(
            num_scalar_prefetch=1,
            grid=(pairs,),
            in_specs=[part(0), part(1), part(2), part(0), whole, whole, whole],
            out_specs=[part(0)] * 4,
            scratch_shapes=[pltpu.VMEM((length, pair), LOW)] * 4
            + [pltpu.VMEM((length, pair), F32)] * 2
            + [pltpu.VMEM((length, pair), LOW), pltpu.VMEM((length, pair), F32)],
        ),
        out_shape=[result] * 4,
        compiler_params=pltpu.CompilerParams(vmem_limit_bytes=56 * 1024 * 1024),
        cost_estimate=pl.CostEstimate(
            flops=pairs * 2 * half_pairs * 12 * 256,
            bytes_accessed=length * width * 24,
            transcendentals=pairs * 2 * half_pairs,
        ),
        name="attention",
    )(order, mixed, mixed, mixed, grad_context, *tables)


class Grid:
    def __init__(self, ctx_n, fsdp_n):
        self.ctx_n, self.fsdp_n = ctx_n, fsdp_n
        self.x_n = 1 << ((ctx_n.bit_length() - 1) // 2)
        self.z_n = ctx_n // self.x_n
        self.core_n = 2 if fsdp_n % 2 == 0 else 1
        self.y_n = fsdp_n // self.core_n
        self.undo = 1 if ctx_n % 3 == 1 else 2

    def locate(self):
        self.ctx, self.fsdp = lax.axis_index("ctx"), lax.axis_index("fsdp")
        self.z, self.x = self.ctx // self.x_n, self.ctx % self.x_n
        self.y, self.core = self.fsdp // self.core_n, self.fsdp % self.core_n
        return self

    def zx(self, dz, dx):
        return ((self.z + dz + self.z_n) % self.z_n) * self.x_n + (
            self.x + dx + self.x_n
        ) % self.x_n

    def yc(self, dy, dc):
        return ((self.y + dy + self.y_n) % self.y_n) * self.core_n + (
            self.core + dc + self.core_n
        ) % self.core_n

    def qkv_piece(self, ctx, fsdp, m):
        span = 3 * self.fsdp_n
        v = (3 * fsdp + m + span * self.ctx_n - ctx * self.fsdp_n) % span
        return ((v // self.fsdp_n) * self.undo) % 3, v % self.fsdp_n

    def qkv_owner(self, ctx, fsdp, m):
        kind, place = self.qkv_piece(ctx, fsdp, m)
        piece = self.ctx_n * self.fsdp_n * kind + ctx * self.fsdp_n + place
        return piece // 3 // self.fsdp_n

    def qkv_user(self, ctx, fsdp, m):
        piece = 3 * (ctx * self.fsdp_n + fsdp) + m
        return (piece % (self.ctx_n * self.fsdp_n)) // self.fsdp_n

    def greet(self):
        barrier = pltpu.get_barrier_semaphore()
        for k in range(1, self.ctx_n):
            pl.semaphore_signal(
                barrier, inc=1, device_id={"ctx": (self.ctx + k) % self.ctx_n}, device_id_type=MESH
            )
        for k in range(1, self.fsdp_n):
            pl.semaphore_signal(
                barrier,
                inc=1,
                device_id={"fsdp": (self.fsdp + k) % self.fsdp_n},
                device_id_type=MESH,
            )
        pl.semaphore_wait(barrier, self.ctx_n + self.fsdp_n - 2)


class Copies:
    def __init__(self, sems):
        self.sems, self.used, self.sent, self.perhaps = sems, 0, [], []

    def sem(self):
        self.used += 1
        return self.sems.at[self.used - 1]

    def send(self, src, dst, **where):
        send_sem, recv_sem = self.sem(), self.sem()
        copy = pltpu.make_async_remote_copy(
            src_ref=src,
            dst_ref=dst,
            send_sem=send_sem,
            recv_sem=recv_sem,
            device_id=where,
            device_id_type=MESH,
        )
        copy.start()
        self.sent.append(copy)
        return recv_sem

    def send_or_keep(self, src, dst, ctx, own_ctx):
        send_sem, recv_sem = self.sem(), self.sem()
        remote = pltpu.make_async_remote_copy(
            src_ref=src,
            dst_ref=dst,
            send_sem=send_sem,
            recv_sem=recv_sem,
            device_id={"ctx": ctx},
            device_id_type=MESH,
        )

        @pl.when(ctx != own_ctx)
        def _():
            remote.start()

        @pl.when(ctx == own_ctx)
        def _():
            pltpu.make_async_copy(src, dst, recv_sem).start()

        self.perhaps.append((ctx != own_ctx, remote))
        return recv_sem

    def local(self, src, dst):
        copy = pltpu.make_async_copy(src, dst, self.sem())
        copy.start()
        return copy

    def drain(self):
        for copy in self.sent:
            copy.wait_send()
        for sent, copy in self.perhaps:

            @pl.when(sent)
            def _(copy=copy):
                copy.wait_send()


def arrived(ref, sem):
    pltpu.make_async_copy(ref, ref, sem).wait()


class TokenGather:
    def __init__(self, grid, copies, own, buffer):
        self.grid, self.copies, self.buffer = grid, copies, buffer
        self.along_x = []
        self.kept = copies.local(own, buffer.at[grid.ctx])
        self.pass_on(own, 0)

    def pass_on(self, src, k):
        grid, copies = self.grid, self.copies
        slot = self.buffer.at[grid.zx(-k, 0)]
        if k < grid.z_n - 1:
            self.along_z = copies.send(src, slot, ctx=grid.zx(1, 0))
        for l in range(1, grid.x_n):
            sem = copies.send(src, slot, ctx=grid.zx(0, l))
            self.along_x.append((k, l, sem))

    def step(self, k):
        slot = self.buffer.at[self.grid.zx(-k, 0)]
        arrived(slot, self.along_z)
        self.pass_on(slot, k)

    def finish(self):
        self.kept.wait()
        for k, l, sem in self.along_x:
            arrived(self.buffer.at[self.grid.zx(-k, -l)], sem)


class ShardGather:
    def __init__(self, grid, copies, own, view):
        self.grid, self.copies, self.view = grid, copies, view
        self.along_y = [
            copies.send(own, view(grid.fsdp), fsdp=grid.yc(k, 0)) for k in range(1, grid.y_n)
        ]
        self.across = []
        self.cross(own, 0)

    def cross(self, src, k):
        for c in range(1, self.grid.core_n):
            slot = self.view(self.grid.yc(-k, 0))
            self.across.append((k, c, self.copies.send(src, slot, fsdp=self.grid.yc(0, c))))

    def forward(self):
        for k in range(1, self.grid.y_n):
            slot = self.view(self.grid.yc(-k, 0))
            arrived(slot, self.along_y[k - 1])
            self.cross(slot, k)

    def finish(self):
        for k, c, sem in self.across:
            arrived(self.view(self.grid.yc(-k, -c)), sem)


def gather_kernel(
    shape, x_in, g_in, wq_in, wu_in, wf_in, wd_in, small_in,
    x_out, g_out, wi_out, wu_out, wo_out, small_out,
    x_s, g_s, wi_s, wu_s, wo_s, small_s, sems,
):
    grid = Grid(*shape).locate()
    copies = Copies(sems)
    unit = wd_in.shape[0]
    fw, dw = wf_in.shape[1] // grid.ctx_n, wd_in.shape[1] // grid.ctx_n
    grid.greet()

    tokens_x = TokenGather(grid, copies, x_in, x_s)
    kept = [
        copies.local(wu_in, wu_s.at[grid.fsdp]),
        copies.local(small_in, small_s.at[grid.ctx, grid.fsdp]),
    ]
    up = ShardGather(grid, copies, wu_in, lambda f: wu_s.at[f])
    peers = [(k, l) for k in range(grid.z_n) for l in range(grid.x_n) if k or l]
    small_sems = [
        copies.send(small_in, small_s.at[grid.ctx, grid.fsdp], ctx=grid.zx(k, l))
        for k, l in peers
    ]
    qkv_sems = []
    for m in range(3):
        user = grid.qkv_user(grid.ctx, grid.fsdp, m)
        kind, place = grid.qkv_piece(user, grid.fsdp, m)
        qkv_sems.append(
            copies.send_or_keep(
                wq_in.at[pl.ds(m * unit, unit)], wi_s.at[kind, place], user, grid.ctx
            )
        )
    tokens_x.step(1)

    def column_block(ref, index, width):
        return ref.at[:, pl.ds(pl.multiple_of(index * width, 128), width)]

    mine = wo_s.at[grid.ctx, grid.fsdp]
    own_out = [
        copies.local(column_block(wf_in, grid.ctx, fw), mine.at[:, pl.ds(0, fw)]),
        copies.local(column_block(wd_in, grid.ctx, dw), mine.at[:, pl.ds(fw, dw)]),
    ]
    out_sems = {}
    for k, l in peers:
        target = grid.zx(k, l)
        out_sems[k, l] = (
            copies.send(column_block(wf_in, target, fw), mine.at[:, pl.ds(0, fw)], ctx=target),
            copies.send(column_block(wd_in, target, dw), mine.at[:, pl.ds(fw, dw)], ctx=target),
        )
    for k in range(2, grid.z_n):
        tokens_x.step(k)
    tokens_g = TokenGather(grid, copies, g_in, g_s)
    up.forward()
    pieces = []
    for m in range(3):
        kind, place = grid.qkv_piece(grid.ctx, grid.fsdp, m)
        arrived(wi_s.at[kind, place], qkv_sems[m])

        def piece_view(f, m=m):
            kind, place = grid.qkv_piece(grid.ctx, f, m)
            return wi_s.at[kind, place]

        pieces.append(ShardGather(grid, copies, wi_s.at[kind, place], piece_view))
    tokens_g.step(1)
    for (k, l), sem in zip(peers, small_sems):
        arrived(small_s.at[grid.zx(-k, -l), grid.fsdp], sem)
    kept[1].wait()
    small = ShardGather(grid, copies, small_s.at[:, grid.fsdp], lambda f: small_s.at[:, f])
    shards = []
    for k in range(grid.z_n):
        first = ((grid.z - k + grid.z_n) % grid.z_n) * grid.x_n
        for l in range(grid.x_n):
            slot = wo_s.at[grid.zx(-k, -l), grid.fsdp]
            if k or l:
                arrived(slot.at[:, pl.ds(0, fw)], out_sems[k, l][0])
                arrived(slot.at[:, pl.ds(fw, dw)], out_sems[k, l][1])
            else:
                own_out[0].wait()
                own_out[1].wait()

        def out_view(f, first=first):
            return wo_s.at[pl.ds(first, grid.x_n), f]

        shards.append(ShardGather(grid, copies, out_view(grid.fsdp), out_view))
        if k + 2 < grid.z_n:
            tokens_g.step(k + 2)
    for gather in pieces + [small] + shards:
        gather.forward()
    kept[0].wait()
    up.finish()
    puts = [copies.local(wu_s, wu_out)]
    tokens_x.finish()
    puts.append(copies.local(x_s, x_out))
    for gather in pieces:
        gather.finish()
    puts.append(copies.local(wi_s, wi_out))
    small.finish()
    puts.append(copies.local(small_s, small_out))
    for gather in shards:
        gather.finish()
    puts.append(copies.local(wo_s, wo_out))
    tokens_g.finish()
    puts.append(copies.local(g_s, g_out))
    for put in puts:
        put.wait()
    copies.drain()


def accumulate(dst, *sources):
    if len(dst.shape) == 3:

        @pl.loop(0, dst.shape[0])
        def _(i):
            accumulate(dst.at[i], *[source.at[i] for source in sources])

        return
    rows, step = dst.shape[0], 16

    @pl.loop(0, rows // step)
    def _(i):
        part = pl.ds(pl.multiple_of(i * step, step), step)
        total = sources[0][part, :].astype(F32)
        for source in sources[1:]:
            total = total + source[part, :].astype(F32)
        dst[part, :] = total.astype(dst.dtype)


class TokenScatter:
    def __init__(self, grid, copies, parts, own, from_x, from_z, total):
        self.grid, self.copies, self.own = grid, copies, own
        self.from_x, self.from_z, self.total = from_x, from_z, total
        self.order = list(range(1, grid.z_n)) + [0]
        self.sems = {
            (k, l): copies.send(
                parts.at[grid.zx(-k, l)], from_x.at[k, l - 1], ctx=grid.zx(0, l)
            )
            for k in self.order
            for l in range(1, grid.x_n)
        }
        self.kept = {k: copies.local(parts.at[grid.zx(-k, 0)], own.at[k]) for k in self.order}

    def step(self, k):
        grid = self.grid
        self.kept[k].wait()
        terms = [self.own.at[k]]
        for l in range(1, grid.x_n):
            arrived(self.from_x.at[k, l - 1], self.sems[k, l])
            terms.append(self.from_x.at[k, l - 1])
        before = grid.z_n - 1 if k == 0 else k - 1
        if before > 0:
            arrived(self.from_z.at[before - 1], self.along_z)
            terms.append(self.from_z.at[before - 1])
        accumulate(self.total if k == 0 else self.own.at[k], *terms)
        if k > 0:
            self.along_z = self.copies.send(
                self.own.at[k], self.from_z.at[k - 1], ctx=grid.zx(1, 0)
            )


class ShardScatter:
    def __init__(self, grid, copies, views, own, from_core, from_y):
        self.grid, self.copies = grid, copies
        self.own, self.from_core, self.from_y = own, from_core, from_y
        self.sems, self.kept = {}, {}
        for k in list(range(1, grid.y_n)) + [0]:
            theirs = views(grid.yc(k, 1))
            ours = views(grid.yc(k, 0))
            self.sems[k] = [
                copies.send(src, from_core.at[k, i], fsdp=grid.yc(0, 1))
                for i, src in enumerate(theirs)
            ]
            self.kept[k] = [copies.local(src, own.at[k, i]) for i, src in enumerate(ours)]

    def step(self, k):
        for i in range(len(self.kept[k])):
            self.kept[k][i].wait()
            arrived(self.from_core.at[k, i], self.sems[k][i])
            accumulate(self.own.at[k, i], self.own.at[k, i], self.from_core.at[k, i])
        if k > 0:
            self.sems[k] = self.copies.send(
                self.own.at[k], self.from_y.at[k - 1], fsdp=self.grid.yc(k, 0)
            )

    def finish(self, result):
        for k in range(1, self.grid.y_n):
            arrived(self.from_y.at[k - 1], self.sems[k])
        for i in range(result.shape[0]):
            accumulate(
                result.at[i],
                self.own.at[0, i],
                *[self.from_y.at[k - 1, i] for k in range(1, self.grid.y_n)],
            )


def scatter_kernel(
    shape, po_in, pn_in, gu_in, go_in, gi_in, small_in,
    to_out, tn_out, gu_out, go_out, gi_out, small_out,
    po_own, po_x, po_z, po_sum, pn_own, pn_x, pn_z, pn_sum,
    gu_own, gu_core, gu_y, gu_sum, go_own, go_core, go_y, go_sum, go_got,
    gi_own, gi_core, gi_y, gi_sum, gi_got, small_s, small_core, small_y, small_x, small_z, sems,
):
    grid = Grid(*shape).locate()
    copies = Copies(sems)
    grid.greet()

    def small_sum(step, buffer, small_sems):
        for i, sem in enumerate(small_sems):
            arrived(buffer.at[i], sem)
        accumulate(
            small_s.at[step + 1], small_s.at[step], *[buffer.at[i] for i in range(len(small_sems))]
        )

    small_kept = copies.local(small_in, small_s.at[0])
    small_sems = [
        copies.send(small_in, small_core.at[c - 1], fsdp=grid.yc(0, c))
        for c in range(1, grid.core_n)
    ]
    shards_o = ShardScatter(
        grid, copies, lambda f: [go_in.at[:, f]], go_own, go_core, go_y
    )
    tokens_o = TokenScatter(grid, copies, po_in, po_own, po_x, po_z, po_sum)

    def qkv_views(f):
        return [gi_in.at[grid.qkv_piece(grid.ctx, f, m)] for m in range(3)]

    shards_i = ShardScatter(grid, copies, qkv_views, gi_own, gi_core, gi_y)
    shards_u = ShardScatter(grid, copies, lambda f: [gu_in.at[f]], gu_own, gu_core, gu_y)
    small_kept.wait()
    small_sum(0, small_core, small_sems)
    small_sems = [
        copies.send(small_s.at[1], small_y.at[k - 1], fsdp=grid.yc(k, 0))
        for k in range(1, grid.y_n)
    ]
    rounds = list(range(1, grid.y_n)) + [0]
    for k in rounds:
        shards_o.step(k)
    tokens_o.step(1)
    small_sum(1, small_y, small_sems)
    small_sems = [
        copies.send(small_s.at[2], small_x.at[l - 1], ctx=grid.zx(0, l))
        for l in range(1, grid.x_n)
    ]
    tokens_n = TokenScatter(grid, copies, pn_in, pn_own, pn_x, pn_z, pn_sum)
    for k in rounds:
        shards_i.step(k)
    for k in rounds:
        shards_u.step(k)
    for k in range(2, grid.z_n):
        tokens_o.step(k)
    small_sum(2, small_x, small_sems)
    small_sems = [
        copies.send(small_s.at[3], small_z.at[k - 1], ctx=grid.zx(k, 0))
        for k in range(1, grid.z_n)
    ]
    shards_o.finish(go_sum)
    peers = [(k, l) for k in range(grid.z_n) for l in range(grid.x_n) if k or l]
    own_o = copies.local(go_sum.at[0, grid.ctx], go_got.at[grid.ctx])
    out_sems = [
        copies.send(go_sum.at[0, grid.zx(k, l)], go_got.at[grid.ctx], ctx=grid.zx(k, l))
        for k, l in peers
    ]
    tokens_o.step(0)
    puts = [copies.local(po_sum, to_out)]
    tokens_n.step(1)
    shards_i.finish(gi_sum)
    qkv_sems = []
    for m in range(3):
        owner = grid.qkv_owner(grid.ctx, grid.fsdp, m)
        qkv_sems.append(copies.send_or_keep(gi_sum.at[m], gi_got.at[m], owner, grid.ctx))
    for k in range(2, grid.z_n):
        tokens_n.step(k)
    shards_u.finish(gu_sum)
    puts.append(copies.local(gu_sum.at[0], gu_out))
    small_sum(3, small_z, small_sems)
    puts.append(copies.local(small_s.at[4], small_out))
    tokens_n.step(0)
    puts.append(copies.local(pn_sum, tn_out))
    own_o.wait()
    for (k, l), sem in zip(peers, out_sems):
        arrived(go_got.at[grid.zx(-k, -l)], sem)
    puts.append(copies.local(go_got, go_out))
    for m in range(3):
        arrived(gi_got.at[m], qkv_sems[m])
    puts.append(copies.local(gi_got, gi_out))
    for put in puts:
        put.wait()
    copies.drain()


def solution(mesh):
    shape = mesh.shape["ctx"], mesh.shape["fsdp"]
    ctx_n, fsdp_n = shape
    n = ctx_n * fsdp_n
    plan = Grid(*shape)
    x_n, z_n, core_n, y_n = plan.x_n, plan.z_n, plan.core_n, plan.y_n

    def gather(x_own, g_own, w_qkv, w_fc1, w_fc2, w_dense, small):
        local_len, width = x_own.shape
        unit, hidden_units = w_fc2.shape
        cols = (hidden_units + width) // ctx_n
        shapes = [
            (ctx_n, local_len, width),
            (ctx_n, local_len, width),
            (3, fsdp_n, unit, width),
            (fsdp_n,) + w_fc1.shape,
            (ctx_n, fsdp_n, unit, cols),
            (ctx_n, fsdp_n) + small.shape,
        ]
        anywhere = pl.BlockSpec(memory_space=pl.ANY)
        return pl.pallas_call(
            functools.partial(gather_kernel, shape),
            out_shape=[jax.ShapeDtypeStruct(s, LOW) for s in shapes],
            in_specs=[anywhere] * 7,
            out_specs=[anywhere] * 6,
            scratch_shapes=[pltpu.VMEM(s, LOW) for s in shapes]
            + [pltpu.SemaphoreType.DMA((SEMAPHORES,))],
            compiler_params=pltpu.CompilerParams(
                collective_id=0, has_side_effects=True, vmem_limit_bytes=VMEM_BYTES
            ),
            name="gather",
        )(x_own, g_own, w_qkv, w_fc1, w_fc2, w_dense, small)

    def scatter(po, pn, gu, go, gi, small):
        local_len, width = po.shape[1:]
        up_rows = gu.shape[1]
        unit, cols = go.shape[2:]
        tokens = [
            pltpu.VMEM((z_n, local_len, width), LOW),
            pltpu.VMEM((z_n, x_n - 1, local_len, width), LOW),
            pltpu.VMEM((z_n - 1, local_len, width), LOW),
            pltpu.VMEM((local_len, width), F32),
        ]

        def shards(*block):
            return [
                pltpu.VMEM((y_n,) + block, LOW),
                pltpu.VMEM((y_n,) + block, LOW),
                pltpu.VMEM((max(y_n - 1, 1),) + block, LOW),
                pltpu.VMEM(block, LOW),
            ]

        anywhere = pl.BlockSpec(memory_space=pl.ANY)
        return pl.pallas_call(
            functools.partial(scatter_kernel, shape),
            out_shape=[
                jax.ShapeDtypeStruct((local_len, width), F32),
                jax.ShapeDtypeStruct((local_len, width), F32),
                jax.ShapeDtypeStruct((up_rows, width), LOW),
                jax.ShapeDtypeStruct((ctx_n, unit, cols), LOW),
                jax.ShapeDtypeStruct((3, unit, width), LOW),
                jax.ShapeDtypeStruct(small.shape, F32),
            ],
            in_specs=[anywhere] * 6,
            out_specs=[anywhere] * 6,
            scratch_shapes=tokens
            + tokens
            + shards(1, up_rows, width)
            + shards(1, ctx_n, unit, cols)
            + [pltpu.VMEM((ctx_n, unit, cols), LOW)]
            + shards(3, unit, width)
            + [pltpu.VMEM((3, unit, width), LOW)]
            + [pltpu.VMEM((count,) + small.shape, F32) for count in (5, 1, y_n, x_n, z_n)]
            + [pltpu.SemaphoreType.DMA((SEMAPHORES,))],
            compiler_params=pltpu.CompilerParams(
                collective_id=1, has_side_effects=True, vmem_limit_bytes=VMEM_BYTES
            ),
            name="scatter",
        )(po, pn, gu, go, gi, small)

    def body(
        hidden_in, positions, ln_gain, ln_bias, w_qkv, b_qkv, w_dense, b_dense,
        w_fc1, b_fc1, w_fc2, b_fc2, out_grad,
    ):
        local_len, width = hidden_in.shape[1:]
        hidden_units = w_fc2.shape[1]
        unit = w_dense.shape[0]
        up_rows = w_fc1.shape[0]
        fw, dw = hidden_units // ctx_n, width // ctx_n
        my_ctx = lax.axis_index("ctx")
        me = my_ctx * fsdp_n + lax.axis_index("fsdp")
        length = positions.shape[1]
        x_own, g_own = hidden_in[0], out_grad[0]

        small_sizes = [unit, unit, 3 * unit, unit, up_rows, unit]
        offsets = [sum(small_sizes[:i]) for i in range(len(small_sizes) + 1)]
        small_rows = -(-offsets[-1] // 2048) * 16
        own_small = jnp.concatenate([ln_gain, ln_bias, b_qkv, b_dense, b_fc1, b_fc2])
        own_small = jnp.pad(own_small, (0, small_rows * 128 - offsets[-1])).reshape(-1, 128)
        x_all, g_all, wi, wu, wo, small = gather(
            x_own, g_own, w_qkv, w_fc1, w_fc2, w_dense, own_small
        )
        small = small.reshape(n, small_rows * 128).astype(F32)
        gain, shift, bias_qkv, bias_dense, bias_up, bias_down = (
            small[:, offsets[i] : offsets[i + 1]].reshape(-1) for i in range(6)
        )
        x_all, g_all = x_all.reshape(length, width), g_all.reshape(length, width)
        wi = wi.reshape(3 * fsdp_n * unit, width)
        wu = wu.reshape(fw, width)
        wo = wo.reshape(width, fw + dw)

        def standardize(values):
            wide = values.astype(F32)
            centered = wide - jnp.mean(wide, axis=-1, keepdims=True)
            spread = lax.rsqrt(jnp.mean(centered * centered, axis=-1, keepdims=True) + EPSILON)
            return centered * spread, spread

        xhat_all = standardize(x_all)[0]
        normed = (xhat_all * gain + shift).astype(LOW)

        runs = length // RUN
        rank = positions[0, ::RUN] // RUN
        stored = jnp.arange(runs, dtype=jnp.int32)
        order = jnp.sum(
            jnp.where(rank[None, :] == stored[:, None], stored[None, :], 0), axis=1
        ).astype(jnp.int32)

        upward = dot_nt(normed, wu) + lax.dynamic_slice_in_dim(bias_up, my_ctx * fw, fw)
        activated = gelu_tanh(upward).astype(LOW)
        mixed = dot_nt(normed, wi) + lax.dynamic_index_in_dim(
            bias_qkv.reshape(3, ctx_n, dw), my_ctx, 1, False
        ).reshape(3 * dw)
        grad_hidden = dot_nn(g_all, wo)
        grad_upward = (grad_hidden[:, :fw] * gelu_slope(upward)).astype(LOW)
        grad_context = grad_hidden[:, fw:].astype(LOW)
        context, dq, dk, dv = attention(order, mixed, grad_context)
        grad_mixed = jnp.concatenate([dq, dk, dv], axis=1)
        hidden = jnp.concatenate([activated, context], axis=1)

        partial_out = dot_nt(hidden, wo).astype(LOW)
        partial_wide = dot_nn(grad_mixed, wi) + dot_nn(grad_upward, wu)
        partial_normed = partial_wide.astype(LOW)

        def column_sum(array):
            return jnp.sum(array, axis=0, dtype=F32)

        terms = jnp.concatenate(
            [
                lax.dynamic_update_slice(
                    jnp.zeros((3, ctx_n, dw), F32),
                    column_sum(grad_mixed).reshape(3, 1, dw),
                    (0, my_ctx, 0),
                ).reshape(-1),
                lax.dynamic_update_slice(
                    jnp.zeros((hidden_units,), F32), column_sum(grad_upward), (my_ctx * fw,)
                ),
                column_sum(g_own),
                column_sum(partial_wide * xhat_all),
                column_sum(partial_wide),
            ]
        ).reshape(-1, 128)
        total, grad_normed, grad_up, grad_o, grad_qkv, sums = scatter(
            partial_out.reshape(ctx_n, local_len, width),
            partial_normed.reshape(ctx_n, local_len, width),
            dot_tn(grad_upward, normed).astype(LOW).reshape(fsdp_n, up_rows, width),
            dot_tn(g_all, hidden).astype(LOW).reshape(ctx_n, fsdp_n, unit, fw + dw),
            dot_tn(grad_mixed, normed).astype(LOW).reshape(3, fsdp_n, unit, width),
            terms,
        )
        hidden_out = (total + x_own.astype(F32) + bias_dense + bias_down).astype(LOW)
        xhat, spread = standardize(x_own)
        e = grad_normed * gain
        grad_in = (
            e - jnp.mean(e, axis=-1, keepdims=True)
            - xhat * jnp.mean(e * xhat, axis=-1, keepdims=True)
        ) * spread + g_own.astype(F32)
        grad_o = grad_o.transpose(1, 0, 2).astype(F32)
        sums = sums.reshape(-1)

        def own_slice(start, size):
            return lax.dynamic_slice_in_dim(sums, start + me * size, size)

        after_up = 3 * width + hidden_units
        grad_b_out = own_slice(after_up, unit)
        return (
            hidden_out[None],
            grad_in[None],
            own_slice(after_up + width, unit),
            own_slice(after_up + 2 * width, unit),
            grad_qkv.reshape(3 * unit, width).astype(F32),
            own_slice(0, 3 * unit),
            grad_o[:, :, fw:].reshape(unit, width),
            grad_b_out,
            grad_up.astype(F32),
            own_slice(3 * width, up_rows),
            grad_o[:, :, :fw].reshape(unit, hidden_units),
            grad_b_out,
        )

    tokens, rows, cells = P("fsdp", "ctx", None), P(BOTH, None), P(BOTH)
    return jax.shard_map(
        body,
        mesh=mesh,
        in_specs=(
            tokens, P("fsdp", None), cells, cells, rows, cells, rows, cells,
            rows, cells, rows, cells, tokens,
        ),
        out_specs=(
            tokens, tokens, cells, cells, rows, cells, rows, cells, rows, cells, rows, cells,
        ),
        check_vma=False,
    )
```

time: 3280 us -> 439 us (0.13)
  the two profiles are of different devices: /device:TPU:10 before, /device:TPU:6 now
where the time goes in v1:
time: 439 us; the launch traced here: 431 us
  Pallas kernels  320 us (73%)
  matrix products  65.6 us (15%)
  other arithmetic  22.7 us (5%)
  local copies, waits for them, and re-layouts  21.6 us (5%)
    pallas_call x1, Pallas kernels, scatter(): pl.pallas_call(functools.partial(scatter_kernel, shape), out_shape=[jax.S...  151 us
    pallas_call x1, Pallas kernels, gather(): pl.pallas_call(functools.partial(gather_kernel, shape), out_shape=[jax.Sh...  141 us
    pallas_call x1, Pallas kernels, attention(): pl.pallas_call(attention_kernel, grid_spec=pltpu.PrefetchScalarGridSpec(n...  27.4 us
    dot_general x3, matrix products, dot_nt(): lax.dot_general(a, b, (((1,), (1,)), ((), ())), preferred_element_type=F32)  23 us
    dot_general x3, matrix products, dot_nn(): lax.dot_general(a, b, (((1,), (0,)), ((), ())), preferred_element_type=F32)  21.4 us
    dot_general x3, matrix products, dot_tn(): lax.dot_general(a, b, (((0,), (0,)), ((), ())), preferred_element_type=F32)  21.2 us

profile of v1, /device:TPU:6, one launch (start us, length us, event | category | flops | bytes accessed | tf_op | source)
XLA Modules:
  0.0 431.5 jit_solution(958053197172593600)
XLA Ops:
  0.7 0.8 slice.37
  1.5 0.6 select_reduce_fusion.order_ref
  2.1 1.2 convert_reduce_fusion.3
  3.3 1.3 fusion.16
  4.6 4.1 concatenate.21
  8.7 0.6 pad_bitcast_fusion.small_in
  9.3 1.1 convert_reduce_fusion.4
  10.5 2.0 fusion.22
  12.5 1.7 concatenate.22.cos_ref
  14.3 1.7 concatenate.24.down_ref
  16.0 1.7 concatenate.23.up_ref
  17.8 141.3 %gather.1 = (bf16[8,128,2048]{2,1,0:T(8,128)(2,1)}, bf16[8,128,2048]{2,1,0:T(8,128)(2,1)}, bf16[3,4,64,2048]{3,2,1,0:T(8,128)(2,1)}, bf16[4,256,2048]{2,1,0:T(8,...) custom-call(bf16[128,2048]{1,0:T(8,128)(2,1)} %bitcast.81, bf16[128,2048]{1,0:T(8,128)(2,1)} %bitcast.83, ...), custom_call_target="tpu_custom_call" | custom-call | tf_op jit(solution)/shard_map/gather/pallas_call | solution.py:660
  159.1 3.0 convert_reduce_fusion
  162.1 0.5 copy-done
  162.5 1.2 multiply_reduce_fusion.1
  163.8 0.1 copy.35
  164.0 0.1 fusion.32
  164.0 0.1 reshape_reshape.3
  164.2 0.1 add.160
  164.5 3.7 add_convert_fusion.1
  168.2 5.2 %convolution_add_fusion.1.q_ref.k_ref.v_ref = f32[1024,768]{1,0:T(8,128)} fusion(bf16[1024,2048]{1,0:T(8,128)(2,1)S(1)} %bitcast.84, bf16[768,2048]{1,0:T(8,128)(2,1)S(1)} %bitcast.111, f32[768]{0:T(1024)S(1)} %add.151), kind=kOutput, calls=%fused_computation.28 | convolution fusion | flops 3222011904 | bytes 10488832 | tf_op jit(solution)/shard_map/dot_general | solution.py:36
  173.4 5.6 %fusion.34 = f32[1024,1280]{1,0:T(8,128)S(1)} fusion(bf16[1024,2048]{1,0:T(8,128)(2,1)S(1)} %bitcast.110, bf16[2048,1280]{1,0:T(8,128)(2,1)S(1)} %bitcast.105), kind=kOutput, calls=%fused_computation.89 | convolution fusion | flops 5368709120 | bytes 14680064 | tf_op jit(solution)/shard_map/dot_general | solution.py:40
  179.0 8.7 %convert_reduce_fusion.1 = (f32[1024]{0:T(1024)S(1)}, bf16[1024,1024]{1,0:T(8,128)(2,1)}, bf16[1024,1024]{1,0:T(8,128)(2,1)}) fusion(f32[1024]{0:T(1024)S(1)} %dynamic_slice.22, f32[1024,1280]{1,0:T(8,128)S(1)} %fusion.34, bf16[1024,2048]{1,0:T(8,128)(2,1)S(1)} %bitcast.85, bf16[1024,2048]{1,0:T(8,128)(2,1)S(1)} %bitcast.107), kind=kOutput, calls=%fused_computation.18 | convolution fusion | flops 4320132096 | bytes 16785408 | tf_op jit(solution)/shard_map/dot_general | solution.py:36
  187.7 0.8 slice.60.g_ref
  188.6 27.4 %attention.1 = (bf16[1024,256]{1,0:T(8,128)(2,1)}, bf16[1024,256]{1,0:T(8,128)(2,1)}, bf16[1024,256]{1,0:T(8,128)(2,1)}, bf16[1024,256]{1,0:T(8,128)(2,1)}) custom-call(s32[16]{0:T(128)} %select_reduce_fusion.order_ref, f32[1024,768]{1,0:T(8,128)} %convolution_add_fusion.1.q_ref.k_ref.v_ref, f32[1024,768]{1,0:T(8,128)} %convolution_add_fusion.1.q_ref.k_ref.v_ref, ...), custom_call_target="tpu_custom_call" | custom-call | flops 8053063680 | bytes 6291456 | tf_op jit(solution)/shard_map/attention/pallas_call | solution.py:160
  216.0 9.1 %convolution_convert_fusion.1 = bf16[1024,2048]{1,0:T(8,128)(2,1)} fusion(bf16[2048,1280]{1,0:T(8,128)(2,1)S(1)} %bitcast.106, bf16[1024,256]{1,0:T(8,128)(2,1)} %get-tuple-element.34, bf16[1024,1024]{1,0:T(8,128)(2,1)} %get-tuple-element.52), kind=kOutput, calls=%fused_computation.21 | convolution fusion | flops 5376049152 | bytes 12058624 | tf_op jit(solution)/shard_map/dot_general | solution.py:36
  225.1 0.3 dynamic_update_slice.7
  225.5 0.3 convert_reduce_fusion.2
  225.9 0.2 copy-done.19
  226.1 10.1 %convolution_convert_fusion = bf16[2048,1280]{1,0:T(8,128)(2,1)} fusion(bf16[1024,2048]{1,0:T(8,128)(2,1)} %bitcast.109, bf16[1024,256]{1,0:T(8,128)(2,1)S(1)} %copy-done.19, bf16[1024,1024]{1,0:T(8,128)(2,1)} %get-tuple-element.52), kind=kOutput, calls=%fused_computation.7 | convolution fusion | flops 5376573440 | bytes 12058624 | tf_op jit(solution)/shard_map/dot_general | solution.py:44
  236.2 5.9 %fusion.35 = f32[1024,2048]{1,0:T(8,128)} fusion(bf16[1024,768]{1,0:T(8,128)(2,1)S(1)} %constant_dynamic-update-slice_fusion, bf16[768,2048]{1,0:T(8,128)(2,1)S(1)} %bitcast.112), kind=kOutput, calls=%fused_computation.90 | convolution fusion | flops 3221225472 | bytes 13107200 | tf_op jit(solution)/shard_map/dot_general | solution.py:40
  242.2 1.0 copy-done.18
  243.2 9.9 %fusion.30 = (f32[2048]{0:T(1024)S(1)}, f32[2048]{0:T(1024)S(1)}, bf16[1024,2048]{1,0:T(8,128)(2,1)}, bf16[1024,2048]{1,0:T(8,128)(2,1)S(1)}) fusion(f32[1024]{0:T(1024)S(1)} %get-tuple-element.64, f32[1024]{0:T(1024)S(1)} %get-tuple-element.62, bf16[8,128,2048]{2,1,0:T(8,128)(2,1)S(1)} %copy-done.1, f32[2048]{0:T(1024)S(1)} %add.142, f32[2048]{0:T(1024)S(1)} %mul.199, ...), kind=kOutput, calls=%fused_computation.85 | convolution fusion | flops 4318031872 | bytes 27303936 | tf_op jit(solution)/shard_map/dot_general | solution.py:40
  253.1 4.9 %convolution_convert_fusion.3 = bf16[768,2048]{1,0:T(8,128)(2,1)} fusion(bf16[1024,768]{1,0:T(8,128)(2,1)S(1)} %constant_dynamic-update-slice_fusion, bf16[1024,2048]{1,0:T(8,128)(2,1)S(1)} %get-tuple-element.51), kind=kOutput, calls=%fused_computation.23 | convolution fusion | flops 3222798336 | bytes 8912896 | tf_op jit(solution)/shard_map/dot_general | solution.py:44
  258.0 6.2 %convolution_convert_fusion.2 = bf16[1024,2048]{1,0:T(8,128)(2,1)} fusion(bf16[1024,1024]{1,0:T(8,128)(2,1)S(1)} %copy-done.18, bf16[1024,2048]{1,0:T(8,128)(2,1)S(1)} %get-tuple-element.51), kind=kOutput, calls=%fused_computation.22 | convolution fusion | flops 4297064448 | bytes 10485760 | tf_op jit(solution)/shard_map/dot_general | solution.py:44
  264.2 151.2 %scatter.1 = (f32[128,2048]{1,0:T(8,128)}, f32[128,2048]{1,0:T(8,128)}, bf16[256,2048]{1,0:T(8,128)(2,1)}, bf16[8,64,1280]{2,1,0:T(8,128)(2,1)}, bf16[3,64,2048]{2,1,0:T(8,128)(2,1)}, /*index=5*/f32[160,128]{1,0:T(8,128)}) custom-call(bf16[8,128,2048]{2,1,0:T(8,128)(2,1)} %bitcast.86, bf16[8,128,2048]{2,1,0:T(8,128)(2,1)} %bitcast.87, ...), custom_call_target="tpu_custom_call" | custom-call | tf_op jit(solution)/shard_map/scatter/pallas_call | solution.py:693
  415.5 1.4 fusion.33
  416.8 1.3 dynamic_slice.26
  418.2 1.3 dynamic_slice.28
  419.5 1.7 multiply_reduce_fusion.2
  421.2 3.5 fusion.17
  424.7 1.4 bitcast_convert_fusion
  426.0 1.6 convert_element_type.107
  427.6 0.2 convert_bitcast_fusion
  427.9 0.3 slice_bitcast_fusion
  428.2 1.5 copy.30
  429.6 0.8 copy.29
  430.5 0.5 copy.45
  (76 shorter events, 0.8 us)
Async XLA Ops:
  159.1 3.5 copy-start
  159.1 4.7 %copy-start.11 = (bf16[8,4,16,128]{3,2,1,0:T(8,128)(2,1)S(1)}, bf16[8,4,16,128]{3,2,1,0:T(8,128)(2,1)}, u32[]{:S(2)}) copy-start(bf16[8,4,16,128]{3,2,1,0:T(8,128)(2,1)} %get-tuple-element.29) | copy-start | bytes 393220
  164.5 3.7 copy-start.16
  164.5 8.9 %slice-start = ((s8[5242880]{0:T(1024)(128)(4,1)}), s8[4194304]{0:T(1024)(128)(4,1)S(1)}, s32[]{:S(2)}) async-start(s8[5242880]{0:T(1024)(128)(4,1)} %bitcast.103), calls=%async_computation | async-start | bytes 8388608
  168.2 5.2 %slice-start.1 = ((s8[5242880]{0:T(1024)(128)(4,1)}), s8[1048576]{0:T(1024)(128)(4,1)S(1)}, s32[]{:S(2)}) async-start(s8[5242880]{0:T(1024)(128)(4,1)} %bitcast.103), calls=%async_computation.1 | async-start | bytes 2097152
  168.2 5.2 %copy-start.15 = (bf16[8,128,2048]{2,1,0:T(8,128)(2,1)S(1)}, bf16[8,128,2048]{2,1,0:T(8,128)(2,1)}, u32[]{:S(2)}) copy-start(bf16[8,128,2048]{2,1,0:T(8,128)(2,1)} %get-tuple-element.32) | copy-start | bytes 12582916
  173.4 5.6 %copy-start.13 = (bf16[4,256,2048]{2,1,0:T(8,128)(2,1)S(1)}, bf16[4,256,2048]{2,1,0:T(8,128)(2,1)}, u32[]{:S(2)}) copy-start(bf16[4,256,2048]{2,1,0:T(8,128)(2,1)} %get-tuple-element.30) | copy-start | bytes 12582916
  216.0 9.4 %copy-start.9 = (bf16[1024,256]{1,0:T(8,128)(2,1)S(1)}, bf16[1024,256]{1,0:T(8,128)(2,1)}, u32[]{:S(2)}) copy-start(bf16[1024,256]{1,0:T(8,128)(2,1)} %get-tuple-element.35) | copy-start | bytes 1572868
  216.0 9.4 %copy-start.8 = (bf16[1024,256]{1,0:T(8,128)(2,1)S(1)}, bf16[1024,256]{1,0:T(8,128)(2,1)}, u32[]{:S(2)}) copy-start(bf16[1024,256]{1,0:T(8,128)(2,1)} %get-tuple-element.36) | copy-start | bytes 1572868
  216.0 9.5 %copy-start.7 = (bf16[1024,256]{1,0:T(8,128)(2,1)S(1)}, bf16[1024,256]{1,0:T(8,128)(2,1)}, u32[]{:S(2)}) copy-start(bf16[1024,256]{1,0:T(8,128)(2,1)} %get-tuple-element.37) | copy-start | bytes 1572868
  225.1 1.0 copy-start.19
  226.1 10.1 %copy-start.17 = (bf16[3,4,64,2048]{3,2,1,0:T(8,128)(2,1)S(1)}, bf16[3,4,64,2048]{3,2,1,0:T(8,128)(2,1)}, u32[]{:S(2)}) copy-start(bf16[3,4,64,2048]{3,2,1,0:T(8,128)(2,1)} %get-tuple-element.31) | copy-start | bytes 9437188
  236.2 6.0 %copy-start.1 = (bf16[8,128,2048]{2,1,0:T(8,128)(2,1)S(1)}, bf16[8,128,2048]{2,1,0:T(8,128)(2,1)}, u32[]{:S(2)}) copy-start(bf16[8,128,2048]{2,1,0:T(8,128)(2,1)} %get-tuple-element.28) | copy-start | bytes 12582916
  236.2 6.0 %copy-start.14 = (bf16[4,256,2048]{2,1,0:T(8,128)(2,1)S(1)}, bf16[4,256,2048]{2,1,0:T(8,128)(2,1)}, u32[]{:S(2)}) copy-start(bf16[4,256,2048]{2,1,0:T(8,128)(2,1)} %get-tuple-element.30) | copy-start | bytes 12582916
  236.2 6.9 %copy-start.18 = (bf16[1024,1024]{1,0:T(8,128)(2,1)S(1)}, bf16[1024,1024]{1,0:T(8,128)(2,1)}, u32[]{:S(2)}) copy-start(bf16[1024,1024]{1,0:T(8,128)(2,1)} %get-tuple-element.49) | copy-start | bytes 6291460
  253.1 4.9 %copy-start.10 = (f32[20480]{0:T(1024)}, f32[20480]{0:T(1024)S(1)}, u32[]{:S(2)}) copy-start(f32[20480]{0:T(1024)S(1)} %constant_dynamic-update-slice_fusion.4) | copy-start | bytes 245764
  264.2 155.3 %copy-start.2 = (bf16[1,128,2048]{2,1,0:T(8,128)(2,1)S(1)}, bf16[1,128,2048]{2,1,0:T(8,128)(2,1)}, u32[]{:S(2)}) copy-start(bf16[1,128,2048]{2,1,0:T(8,128)(2,1)} %param.13) | copy-start | bytes 1572868
  264.2 156.9 %copy-start.3 = (bf16[1,128,2048]{2,1,0:T(8,128)(2,1)S(1)}, bf16[1,128,2048]{2,1,0:T(8,128)(2,1)}, u32[]{:S(2)}) copy-start(bf16[1,128,2048]{2,1,0:T(8,128)(2,1)} %param.25) | copy-start | bytes 1572868
  415.5 9.2 %copy-start.6 = (bf16[3,64,2048]{2,1,0:T(8,128)(2,1)S(1)}, bf16[3,64,2048]{2,1,0:T(8,128)(2,1)}, u32[]{:S(2)}) copy-start(bf16[3,64,2048]{2,1,0:T(8,128)(2,1)} %get-tuple-element.41) | copy-start | bytes 2359300
  416.8 13.6 %copy-start.12 = (f32[64]{0:T(128)}, f32[64]{0:T(128)S(1)}, u32[]{:S(2)}) copy-start(f32[64]{0:T(128)S(1)} %get-tuple-element.95) | copy-start | bytes 772
  419.5 6.5 %copy-start.5 = (bf16[256,2048]{1,0:T(8,128)(2,1)S(1)}, bf16[256,2048]{1,0:T(8,128)(2,1)}, u32[]{:S(2)}) copy-start(bf16[256,2048]{1,0:T(8,128)(2,1)} %get-tuple-element.43) | copy-start | bytes 3145732
  421.2 6.4 %copy-start.4 = (bf16[8,64,1280]{2,1,0:T(8,128)(2,1)S(1)}, bf16[8,64,1280]{2,1,0:T(8,128)(2,1)}, u32[]{:S(2)}) copy-start(bf16[8,64,1280]{2,1,0:T(8,128)(2,1)} %get-tuple-element.42) | copy-start | bytes 3932164

commit v2 on v1

v2 whole, which is shorter than its diff:
```python
import functools

import jax
import jax.numpy as jnp
import numpy as np
from jax import lax
from jax.experimental import pallas as pl
from jax.experimental.pallas import tpu as pltpu
from jax.sharding import PartitionSpec as P

HEAD_DIM = 64
ROT_DIM = 32
RUN = 64
EPSILON = 1e-05
SCORE_SCALE = 0.125
BOTH = ("ctx", "fsdp")
F32 = jnp.float32
LOW = jnp.bfloat16
MESH = pl.DeviceIdType.MESH
SEMAPHORES = 512
VMEM_BYTES = 60 * 1024 * 1024
SMALL_ROWS = (
    [(row, (1, 0)) for row in range(4)]
    + [(4, (3, j)) for j in range(3)]
    + [(7, (4, j)) for j in range(4)]
)


def dot_nt(a, b):
    return lax.dot_general(a, b, (((1,), (1,)), ((), ())), preferred_element_type=F32)


def dot_nn(a, b):
    return lax.dot_general(a, b, (((1,), (0,)), ((), ())), preferred_element_type=F32)


def dot_tn(a, b):
    return lax.dot_general(a, b, (((0,), (0,)), ((), ())), preferred_element_type=F32)


def turning_tables(length):
    half_rot = ROT_DIM // 2
    lane = np.arange(2 * HEAD_DIM) % HEAD_DIM
    freqs = np.where(lane < ROT_DIM, 10000.0 ** (-(lane % half_rot) / half_rot), 0.0)
    starts = np.arange(0, length, RUN)[:, None] * freqs[None, :]
    steps = np.arange(RUN)[:, None] * freqs[None, :]
    return (
        np.stack([np.cos(starts), np.sin(starts)]).astype(np.float32),
        np.stack([np.cos(steps), np.sin(steps)]).astype(np.float32),
    )


def run_turn(start_ref, step_ref, run):
    lane = lax.broadcasted_iota(jnp.int32, (RUN, 2 * HEAD_DIM), 1) % HEAD_DIM
    half_rot = ROT_DIM // 2
    cos_a, sin_a = start_ref[0, pl.ds(run, 1), :], start_ref[1, pl.ds(run, 1), :]
    cos_b, sin_b = step_ref[0], step_ref[1]
    cosine = cos_a * cos_b - sin_a * sin_b
    sine = sin_a * cos_b + cos_a * sin_b
    above = jnp.where(lane < half_rot, -sine, 0.0)
    below = jnp.where((lane >= half_rot) & (lane < ROT_DIM), sine, 0.0)
    return cosine, above, below


def turn(u, tables, way=1.0):
    cosine, above, below = tables
    half_rot = ROT_DIM // 2
    width = 2 * HEAD_DIM
    moved = pltpu.roll(u, width - half_rot, 1) * above + pltpu.roll(u, half_rot, 1) * below
    return u * cosine + way * moved


def masked_tile(scores, diagonal, start):
    last = jnp.where(diagonal, scores[:, start:], -1e30)
    return jnp.concatenate([scores[:, :start], last], axis=1) if start > 0 else last


def lower_triangle(tile):
    return lax.broadcasted_iota(jnp.int32, (tile, tile), 1) <= lax.broadcasted_iota(
        jnp.int32, (tile, tile), 0
    )


def head_lanes(tile, head):
    lanes = lax.broadcasted_iota(jnp.int32, (tile, 2 * HEAD_DIM), 1)
    return (lanes // HEAD_DIM) == head


def pick(mine, values):
    return jnp.where(mine, values, jnp.zeros_like(values))


def attend(q_s, k_s, v_s, ctx_s, lse_s):
    length = q_s.shape[0]
    tile = min(256, length)
    diagonal = lower_triangle(tile)
    for start in range(0, length, tile):
        rows, reach = slice(start, start + tile), start + tile
        context = jnp.zeros((tile, 2 * HEAD_DIM), F32)
        lse = jnp.zeros((tile, 2 * HEAD_DIM), F32)
        for head in range(2):
            mine = head_lanes(tile, head)
            scores = dot_nt(pick(mine, q_s[rows, :]), k_s[:reach, :])
            scores = masked_tile(scores, diagonal, start)
            peak = jnp.max(scores, axis=1, keepdims=True)
            exps = jnp.exp(scores - peak)
            total = jnp.sum(exps, axis=1, keepdims=True)
            probs_low = (exps * (1.0 / total)).astype(LOW)
            context = jnp.where(mine, dot_nn(probs_low, v_s[:reach, :]), context)
            lse = jnp.where(mine, peak + jnp.log(total), lse)
        ctx_s[rows, :] = context.astype(LOW)
        lse_s[rows, :] = lse


class Grid:
    def __init__(self, ctx_n, fsdp_n):
        self.ctx_n, self.fsdp_n = ctx_n, fsdp_n
        self.x_n = 1 << ((ctx_n.bit_length() - 1) // 2)
        self.z_n = ctx_n // self.x_n
        self.core_n = 2 if fsdp_n % 2 == 0 else 1
        self.y_n = fsdp_n // self.core_n
        self.undo = 1 if ctx_n % 3 == 1 else 2

    def locate(self):
        self.ctx, self.fsdp = lax.axis_index("ctx"), lax.axis_index("fsdp")
        self.z, self.x = self.ctx // self.x_n, self.ctx % self.x_n
        self.y, self.core = self.fsdp // self.core_n, self.fsdp % self.core_n
        return self

    def zx(self, dz, dx):
        return ((self.z + dz + self.z_n) % self.z_n) * self.x_n + (
            self.x + dx + self.x_n
        ) % self.x_n

    def yc(self, dy, dc):
        return ((self.y + dy + self.y_n) % self.y_n) * self.core_n + (
            self.core + dc + self.core_n
        ) % self.core_n

    def nearest(self, j):
        place = 0
        for z in range(self.z_n):
            order = sorted(range(self.z_n), key=lambda other: (abs(other - z), other))
            place = place + jnp.where(self.z == z, order[j], 0)
        return place

    def qkv_piece(self, ctx, fsdp, m):
        span = 3 * self.fsdp_n
        v = (3 * fsdp + m + span * self.ctx_n - ctx * self.fsdp_n) % span
        return ((v // self.fsdp_n) * self.undo) % 3, v % self.fsdp_n

    def qkv_owner(self, ctx, fsdp, m):
        kind, place = self.qkv_piece(ctx, fsdp, m)
        piece = self.ctx_n * self.fsdp_n * kind + ctx * self.fsdp_n + place
        return piece // 3 // self.fsdp_n

    def qkv_user(self, ctx, fsdp, m):
        piece = 3 * (ctx * self.fsdp_n + fsdp) + m
        return (piece % (self.ctx_n * self.fsdp_n)) // self.fsdp_n

    def greet(self):
        barrier = pltpu.get_barrier_semaphore()
        for k in range(1, self.ctx_n):
            pl.semaphore_signal(
                barrier, inc=1, device_id={"ctx": (self.ctx + k) % self.ctx_n}, device_id_type=MESH
            )
        for k in range(1, self.fsdp_n):
            pl.semaphore_signal(
                barrier,
                inc=1,
                device_id={"fsdp": (self.fsdp + k) % self.fsdp_n},
                device_id_type=MESH,
            )
        pl.semaphore_wait(barrier, self.ctx_n + self.fsdp_n - 2)


class Copies:
    def __init__(self, sems):
        self.sems, self.used, self.sent, self.perhaps = sems, 0, [], []

    def sem(self):
        self.used += 1
        return self.sems.at[self.used - 1]

    def send(self, src, dst, **where):
        send_sem, recv_sem = self.sem(), self.sem()
        copy = pltpu.make_async_remote_copy(
            src_ref=src,
            dst_ref=dst,
            send_sem=send_sem,
            recv_sem=recv_sem,
            device_id=where,
            device_id_type=MESH,
        )
        copy.start()
        self.sent.append(copy)
        return recv_sem

    def send_or_keep(self, src, dst, ctx, own_ctx):
        send_sem, recv_sem = self.sem(), self.sem()
        remote = pltpu.make_async_remote_copy(
            src_ref=src,
            dst_ref=dst,
            send_sem=send_sem,
            recv_sem=recv_sem,
            device_id={"ctx": ctx},
            device_id_type=MESH,
        )

        @pl.when(ctx != own_ctx)
        def _():
            remote.start()

        @pl.when(ctx == own_ctx)
        def _():
            pltpu.make_async_copy(src, dst, recv_sem).start()

        self.perhaps.append((ctx != own_ctx, remote))
        return recv_sem

    def prepare(self, src, dst, **where):
        send_sem, recv_sem = self.sem(), self.sem()
        remote = pltpu.make_async_remote_copy(
            src_ref=src,
            dst_ref=dst,
            send_sem=send_sem,
            recv_sem=recv_sem,
            device_id=where,
            device_id_type=MESH,
        )
        return remote, recv_sem

    def start_if(self, when, remote):
        @pl.when(when)
        def _():
            remote.start()

        self.perhaps.append((when, remote))

    def send_if(self, when, src, dst, **where):
        remote, recv_sem = self.prepare(src, dst, **where)
        self.start_if(when, remote)
        return recv_sem

    def local(self, src, dst):
        copy = pltpu.make_async_copy(src, dst, self.sem())
        copy.start()
        return copy

    def drain(self):
        for copy in self.sent:
            copy.wait_send()
        for sent, copy in self.perhaps:

            @pl.when(sent)
            def _(copy=copy):
                copy.wait_send()


def arrived(ref, sem):
    pltpu.make_async_copy(ref, ref, sem).wait()


class TokenGather:
    def __init__(self, grid, copies, own, buffer):
        self.grid, self.copies, self.buffer = grid, copies, buffer
        self.rows = own.shape[0]
        self.across = []
        self.kept = copies.local(own, self.slot(0, 0))
        self.along = {
            way: copies.send_if(self.ends(way), own, self.slot(0, 0), ctx=grid.zx(way, 0))
            for way in (1, -1)
        }
        for l in range(1, grid.x_n):
            sem = copies.send(own, self.slot(0, 0), ctx=grid.zx(0, l))
            self.across.append((0, 1, l, sem))

    def slot(self, k, l):
        start = pl.multiple_of(self.grid.zx(-k, -l) * self.rows, self.rows)
        return self.buffer.at[pl.ds(start, self.rows)]

    def ends(self, way):
        return self.grid.z < self.grid.z_n - 1 if way > 0 else self.grid.z > 0

    def has(self, k, way):
        z = self.grid.z
        return z >= k if way > 0 else z + k < self.grid.z_n

    def step(self, k):
        grid, copies, along = self.grid, self.copies, {}
        for way in (1, -1):
            slot, here = self.slot(k * way, 0), self.has(k, way)

            @pl.when(here)
            def _(slot=slot, way=way):
                arrived(slot, self.along[way])

            if k < grid.z_n - 1:
                along[way] = copies.send_if(
                    here & self.ends(way), slot, slot, ctx=grid.zx(way, 0)
                )
            for l in range(1, grid.x_n):
                sem = copies.send_if(here, slot, slot, ctx=grid.zx(0, l))
                self.across.append((k, way, l, sem))
        self.along = along

    def ready(self, k):
        if k == 0:
            self.kept.wait()
        for m, way, l, sem in self.across:
            if m == k:

                @pl.when(self.has(k, way))
                def _(way=way, l=l, sem=sem):
                    arrived(self.slot(k * way, l), sem)


class ShardGather:
    def __init__(self, grid, copies, own, view):
        self.grid, self.copies, self.view = grid, copies, view
        self.along_y = [
            copies.send(own, view(grid.fsdp), fsdp=grid.yc(k, 0)) for k in range(1, grid.y_n)
        ]
        self.across = []
        self.cross(own, 0)

    def cross(self, src, k):
        for c in range(1, self.grid.core_n):
            slot = self.view(self.grid.yc(-k, 0))
            self.across.append((k, c, self.copies.send(src, slot, fsdp=self.grid.yc(0, c))))

    def forward(self):
        for k in range(1, self.grid.y_n):
            slot = self.view(self.grid.yc(-k, 0))
            arrived(slot, self.along_y[k - 1])
            self.cross(slot, k)

    def finish(self):
        for k, c, sem in self.across:
            arrived(self.view(self.grid.yc(-k, -c)), sem)


def gather_kernel(
    shape, x_in, g_in, wq_in, wu_in, wf_in, wd_in,
    small_in, row_in, column_in, start_in, step_in,
    x_out, g_out, wi_out, wu_out, wo_out, small_out, normed_out, hidden_out, slope_out,
    qkv_out, lse_out, stats_out,
    x_s, g_s, wi_s, wu_s, wo_s, normed_s, hidden_s, slope_s, qkv_s, lse_s, stats_s,
    mixed_s, ctx_s, small_f, qkv_bias_s, up_bias_s, small_s, small_x, small_core, small_y, small_z, sems,
):
    grid = Grid(*shape).locate()
    copies = Copies(sems)
    local_len, width = x_in.shape
    unit, up_rows = wd_in.shape[0], wu_in.shape[0]
    fw, dw = wf_in.shape[1] // grid.ctx_n, wd_in.shape[1] // grid.ctx_n
    n = grid.ctx_n * grid.fsdp_n
    me = grid.ctx * grid.fsdp_n + grid.fsdp
    peers = [(k, l) for k in range(grid.z_n) for l in range(grid.x_n) if k or l]
    pairs = dw // (2 * HEAD_DIM)
    puts = []

    row_index = lax.broadcasted_iota(jnp.int32, (16, width), 0)
    placed = jnp.zeros((16, width), F32)
    pieces_in = small_in[...].astype(F32)
    for row, (base, each) in enumerate(SMALL_ROWS):
        piece = each[0] * me + each[1]
        value = jnp.broadcast_to(pieces_in[row : row + 1, :], (16, width))
        value = pltpu.roll(value, (piece % n) * unit, 1)
        placed = placed + jnp.where(row_index == piece // n + base, value, 0.0)
    small_s[0] = placed.astype(LOW)
    grid.greet()

    def small_sum(step, buffer, stage):
        for i, sem in enumerate(stage):
            arrived(buffer.at[i], sem)
        accumulate(
            small_s.at[step + 1], small_s.at[step], *[buffer.at[i] for i in range(len(stage))]
        )

    stage = [
        copies.send(small_s.at[0], small_y.at[k - 1], fsdp=grid.yc(k, 0))
        for k in range(1, grid.y_n)
    ]

    def up_slot(f):
        return wu_s.at[pl.ds(pl.multiple_of(f * up_rows, up_rows), up_rows)]

    up_kept = copies.local(wu_in, up_slot(grid.fsdp))
    up = ShardGather(grid, copies, wu_in, up_slot)
    qkv_sems = []

    def piece_slot(ctx, fsdp, m):
        kind, place = grid.qkv_piece(ctx, fsdp, m)
        return wi_s.at[pl.ds(pl.multiple_of((kind * grid.fsdp_n + place) * unit, unit), unit)]

    for m in range(3):
        user = grid.qkv_user(grid.ctx, grid.fsdp, m)
        qkv_sems.append(
            copies.send_or_keep(
                wq_in.at[pl.ds(m * unit, unit)],
                piece_slot(user, grid.fsdp, m),
                user,
                grid.ctx,
            )
        )
    small_sum(0, small_y, stage)
    stage = [
        copies.send(small_s.at[1], small_x.at[l - 1], ctx=grid.zx(0, l))
        for l in range(1, grid.x_n)
    ]
    tokens_x = TokenGather(grid, copies, x_in, x_s)
    small_sum(1, small_x, stage)
    stage = [
        copies.send(small_s.at[2], small_core.at[c - 1], fsdp=grid.yc(0, c))
        for c in range(1, grid.core_n)
    ]
    small_sum(2, small_core, stage)
    stage = [
        copies.send(small_s.at[3], small_z.at[k - 1], ctx=grid.zx(k, 0))
        for k in range(1, grid.z_n)
    ]

    def column_block(ref, index, block):
        return ref.at[:, pl.ds(pl.multiple_of(index * block, 128), block)]

    mine = wo_s.at[grid.ctx, grid.fsdp]
    own_out = [
        copies.local(column_block(wf_in, grid.ctx, fw), mine.at[:, pl.ds(0, fw)]),
        copies.local(column_block(wd_in, grid.ctx, dw), mine.at[:, pl.ds(fw, dw)]),
    ]
    out_sems = {}

    def send_out(k):
        for l in range(grid.x_n):
            if k or l:
                target = grid.zx(k, l)
                out_sems[k, l] = (
                    copies.send(
                        column_block(wf_in, target, fw), mine.at[:, pl.ds(0, fw)], ctx=target
                    ),
                    copies.send(
                        column_block(wd_in, target, dw), mine.at[:, pl.ds(fw, dw)], ctx=target
                    ),
                )

    shards = []

    def spread_out(k):
        first = ((grid.z - k + grid.z_n) % grid.z_n) * grid.x_n
        for l in range(grid.x_n):
            slot = wo_s.at[grid.zx(-k, -l), grid.fsdp]
            if k or l:
                arrived(slot.at[:, pl.ds(0, fw)], out_sems[k, l][0])
                arrived(slot.at[:, pl.ds(fw, dw)], out_sems[k, l][1])
            else:
                own_out[0].wait()
                own_out[1].wait()

        def out_view(f):
            return wo_s.at[pl.ds(first, grid.x_n), f]

        shards.append(ShardGather(grid, copies, out_view(grid.fsdp), out_view))

    group = grid.x_n * local_len

    def group_rows(k):
        return pl.multiple_of(grid.nearest(k) * group, group)

    def normalize(k):
        first = group_rows(k)
        gain, shift = small_f[0:1, :], small_f[1:2, :]

        @pl.loop(0, group // 16)
        def _(i):
            rows = pl.ds(pl.multiple_of(first + i * 16, 16), 16)
            wide = x_s[rows, :].astype(F32)
            mean = jnp.mean(wide, axis=-1, keepdims=True)
            centered = wide - mean
            spread = lax.rsqrt(jnp.mean(centered * centered, axis=-1, keepdims=True) + EPSILON)
            normed_s[rows, :] = (centered * spread * gain + shift).astype(LOW)
            lane = lax.broadcasted_iota(jnp.int32, (16, 2 * HEAD_DIM), 1)
            stats_s[rows, :] = jnp.where(lane < HEAD_DIM, mean, spread)

    tile_rows = min(256, group)

    def project_up(k):
        first = group_rows(k)
        block = min(256, fw)

        @pl.loop(0, (group // tile_rows) * (fw // block))
        def _(i):
            part, col = i // (fw // block), (i % (fw // block)) * block
            rows = pl.ds(pl.multiple_of(first + part * tile_rows, tile_rows), tile_rows)
            cols = pl.ds(pl.multiple_of(col, block), block)
            bias = up_bias_s[i % (fw // block), 0:1, :]
            upward = dot_nt(normed_s[rows, :], wu_s[cols, :]) + bias
            square = upward * upward
            bend = jnp.tanh(0.7978845608028654 * (upward + 0.044715 * square * upward))
            half = 0.5 * (1.0 + bend)
            hidden_s[rows, cols] = (upward * half).astype(LOW)
            inner_slope = 0.7978845608028654 * (1.0 + 3.0 * 0.044715 * square)
            slope = half + 0.5 * upward * (1.0 - bend * bend) * inner_slope
            slope_s[rows, cols] = slope.astype(LOW)

    def project_qkv(k):
        first = group_rows(k)

        @pl.loop(0, group // tile_rows)
        def _(i):
            start = pl.multiple_of(first + i * tile_rows, tile_rows)
            rows = pl.ds(start, tile_rows)
            for kind in range(3):
                result = dot_nt(normed_s[rows, :], wi_s[kind * dw : (kind + 1) * dw, :])
                result = result + qkv_bias_s[kind, 0:1, :]
                if kind == 2:
                    mixed_s[rows, kind * dw : (kind + 1) * dw] = result.astype(LOW)
                    continue
                for run in range(tile_rows // RUN):
                    tables = run_turn(start_in, step_in, start // RUN + run)
                    run_at = pl.ds(pl.multiple_of(start + run * RUN, RUN), RUN)
                    for p in range(pairs):
                        lanes = slice(p * 2 * HEAD_DIM, (p + 1) * 2 * HEAD_DIM)
                        turned = turn(result[run * RUN : (run + 1) * RUN, lanes], tables)
                        low = turned.astype(LOW)
                        if kind == 0:
                            low = (low * SCORE_SCALE).astype(LOW)
                        at = kind * dw + p * 2 * HEAD_DIM
                        mixed_s[run_at, at : at + 2 * HEAD_DIM] = low

    for k in range(grid.z_n):
        send_out(k)
    tokens_g = TokenGather(grid, copies, g_in, g_s)
    tokens_x.step(1)
    pieces = []
    for m in range(3):
        arrived(piece_slot(grid.ctx, grid.fsdp, m), qkv_sems[m])
        pieces.append(
            ShardGather(
                grid,
                copies,
                piece_slot(grid.ctx, grid.fsdp, m),
                lambda f, m=m: piece_slot(grid.ctx, f, m),
            )
        )
    up.forward()
    small_sum(3, small_z, stage)
    puts.append(copies.local(small_s.at[4], small_out))
    small_f[...] = small_s[4].astype(F32)
    for kind in range(3):
        at = pl.ds(pl.multiple_of(grid.ctx * dw, 128), dw)
        row = small_f[4 + kind : 5 + kind, at]
        qkv_bias_s[kind] = jnp.broadcast_to(row, qkv_bias_s.shape[1:])
    block = up_bias_s.shape[2]
    for i in range(fw // block):
        offset = grid.ctx * fw
        at = pl.ds(pl.multiple_of(offset % width + i * block, 128), block)
        row = jnp.zeros((1, block), F32)
        for j in range(4):
            row = row + jnp.where(offset // width == j, small_f[7 + j : 8 + j, at], 0.0)
        up_bias_s[i] = jnp.broadcast_to(row, up_bias_s.shape[1:])
    tokens_x.ready(0)
    normalize(0)
    up_kept.wait()
    up.finish()
    puts.append(copies.local(wu_s, wu_out))
    project_up(0)
    for gather in pieces:
        gather.forward()
    spread_out(0)
    tokens_x.ready(1)
    normalize(1)
    project_up(1)
    for gather in pieces:
        gather.finish()
    puts.append(copies.local(wi_s, wi_out))
    project_qkv(0)
    project_qkv(1)
    tokens_g.step(1)
    for k in range(2, grid.z_n):
        tokens_x.step(k)
        spread_out(k - 1)
        tokens_g.step(k)
        shards[k - 2].forward()
    spread_out(grid.z_n - 1)
    shards[grid.z_n - 2].forward()
    for k in range(2, grid.z_n):
        tokens_x.ready(k)
        normalize(k)
        project_up(k)
        project_qkv(k)
        if k == 2:
            shards[grid.z_n - 1].forward()
    puts.append(copies.local(x_s, x_out))
    puts.append(copies.local(normed_s, normed_out))
    puts.append(copies.local(slope_s, slope_out))
    puts.append(copies.local(stats_s, stats_out))
    length = x_s.shape[0]
    pair = 2 * HEAD_DIM

    tall = min(256, length)

    @pl.loop(0, length // tall)
    def _(i):
        start = pl.multiple_of(i * tall, tall)
        result = dot_nn(to_sorted(row_in, start, tall), mixed_s[...]).astype(LOW)
        for kind in range(3):
            for p in range(pairs):
                at = kind * dw + p * pair
                qkv_s[kind, p, pl.ds(start, tall), :] = result[:, at : at + pair]

    @pl.loop(0, pairs)
    def _(p):
        attend(qkv_s.at[0, p], qkv_s.at[1, p], qkv_s.at[2, p], ctx_s.at[p], lse_s.at[p])

    @pl.loop(0, length // tall)
    def _(i):
        start = pl.multiple_of(i * tall, tall)
        back = to_stored(column_in, start, tall)
        for p in range(pairs):
            at = slice(fw + p * pair, fw + (p + 1) * pair)
            hidden_s[pl.ds(start, tall), at] = dot_nn(back, ctx_s[p]).astype(LOW)

    puts.append(copies.local(hidden_s, hidden_out))
    puts.append(copies.local(qkv_s, qkv_out))
    puts.append(copies.local(lse_s, lse_out))
    for gather in shards:
        gather.finish()
    puts.append(copies.local(wo_s, wo_out))
    for k in range(grid.z_n):
        tokens_g.ready(k)
    puts.append(copies.local(g_s, g_out))
    for put in puts:
        put.wait()
    copies.drain()


def accumulate(dst, *sources):
    if len(dst.shape) == 3:

        @pl.loop(0, dst.shape[0])
        def _(i):
            accumulate(dst.at[i], *[source.at[i] for source in sources])

        return
    rows, step = dst.shape[0], 16

    @pl.loop(0, rows // step)
    def _(i):
        part = pl.ds(pl.multiple_of(i * step, step), step)
        total = sources[0][part, :].astype(F32)
        for source in sources[1:]:
            total = total + source[part, :].astype(F32)
        dst[part, :] = total.astype(dst.dtype)


class TokenScatter:
    def __init__(self, grid, copies, parts, from_x, from_z, total):
        self.grid, self.copies, self.parts = grid, copies, parts
        self.from_x, self.from_z, self.total = from_x, from_z, total
        self.rows = total.shape[0]
        self.along_x, self.sems = {}, {}
        self.order = [t for i in range(grid.z_n // 2) for t in (grid.z_n - 1 - i, i)]

    def block(self, t, dx):
        x = (self.grid.x + dx) % self.grid.x_n
        return self.parts.at[t, pl.ds(pl.multiple_of(x * self.rows, self.rows), self.rows)]

    def launch(self, t):
        for l in range(1, self.grid.x_n):
            self.along_x[t, l] = self.copies.send(
                self.block(t, l), self.from_x.at[t, l - 1], ctx=self.grid.zx(0, l)
            )

    def collect(self, t):
        terms = [self.block(t, 0)]
        for l in range(1, self.grid.x_n):
            arrived(self.from_x.at[t, l - 1], self.along_x[t, l])
            terms.append(self.from_x.at[t, l - 1])
        accumulate(terms[0], *terms)

    def climb(self, t):
        grid, own, slot = self.grid, self.block(t, 0), self.from_z.at[t]
        remote, sem = self.copies.prepare(own, slot, ctx=grid.zx(1, 0))

        @pl.when((grid.z < t) & (grid.z > 0))
        def _():
            arrived(slot, sem)
            accumulate(own, own, slot)

        self.copies.start_if(grid.z < t, remote)
        self.sems[t, 1] = sem

    def descend(self, t):
        grid, own, slot = self.grid, self.block(t, 0), self.from_z.at[t]
        there = self.from_z.at[jnp.where(grid.z - 1 == t, grid.z_n, t)]
        remote, sem = self.copies.prepare(own, there, ctx=grid.zx(-1, 0))

        @pl.when((grid.z > t) & (grid.z < grid.z_n - 1))
        def _():
            arrived(slot, sem)
            accumulate(own, own, slot)

        self.copies.start_if(grid.z > t, remote)
        self.sems[t, -1] = sem

    def step(self, i):
        last = self.grid.z_n - 1
        self.collect(self.order[i])
        known = self.order[: i + 1]
        for t in range(last, 0, -1):
            ready = [u for u in known if u >= t]
            if len(ready) == last - t + 1 and (t, 1) not in self.sems and t in known:
                self.climb(t)
        for t in range(last):
            ready = [u for u in known if u <= t]
            if len(ready) == t + 1 and (t, -1) not in self.sems and t in known:
                self.descend(t)

    def finish(self):
        grid = self.grid
        for t in range(grid.z_n):

            @pl.when(grid.z == t)
            def _(t=t):
                terms = [self.block(t, 0)]
                if t > 0:
                    arrived(self.from_z.at[t], self.sems[t, 1])
                    terms.append(self.from_z.at[t])
                if t < grid.z_n - 1:
                    arrived(self.from_z.at[grid.z_n], self.sems[t, -1])
                    terms.append(self.from_z.at[grid.z_n])
                accumulate(self.total, *terms)


class ShardScatter:
    def __init__(self, grid, copies, views, from_core, from_y):
        self.grid, self.copies, self.views = grid, copies, views
        self.from_core, self.from_y = from_core, from_y
        self.rounds = list(range(1, grid.y_n)) + [0]
        self.across = {
            k: [
                copies.send(part, from_core.at[k, i], fsdp=grid.yc(0, 1))
                for i, part in enumerate(views(grid.yc(k, 1)))
            ]
            for k in self.rounds
        }
        self.along_y = {}

    def step(self, k):
        for i, part in enumerate(self.views(self.grid.yc(k, 0))):
            arrived(self.from_core.at[k, i], self.across[k][i])
            accumulate(part, part, self.from_core.at[k, i])
            if k > 0:
                self.along_y[k, i] = self.copies.send(
                    part, self.from_y.at[k - 1, i], fsdp=self.grid.yc(k, 0)
                )

    def finish(self):
        for i, part in enumerate(self.views(self.grid.fsdp)):
            for k in range(1, self.grid.y_n):
                arrived(self.from_y.at[k - 1, i], self.along_y[k, i])
            accumulate(
                part, part, *[self.from_y.at[k - 1, i] for k in range(1, self.grid.y_n)]
            )


def to_sorted(row_ref, start, tile):
    length = row_ref.shape[1]
    place = lax.broadcasted_iota(jnp.int32, (tile, length), 0) + start
    return jnp.where(place == row_ref[0:1, :], 1.0, 0.0).astype(LOW)


def to_stored(column_ref, start, tile):
    length = column_ref.shape[0]
    place = lax.broadcasted_iota(jnp.int32, (tile, length), 1)
    return jnp.where(place == column_ref[pl.ds(start, tile), :], 1.0, 0.0).astype(LOW)


def run_rows(i):
    return pl.ds(pl.multiple_of(i * RUN, RUN), RUN)


def attend_back(q_s, k_s, v_s, lse_s, g_s, dq_s, dk_s, dv_s):
    length = q_s.shape[0]
    dk_s[...] = jnp.zeros_like(dk_s)
    dv_s[...] = jnp.zeros_like(dv_s)
    tile = min(256, length)
    diagonal = lower_triangle(tile)
    for start in range(0, length, tile):
        rows, reach = slice(start, start + tile), start + tile
        grad_q = jnp.zeros((tile, 2 * HEAD_DIM), F32)
        for head in range(2):
            mine = head_lanes(tile, head)
            q_own, g_own = pick(mine, q_s[rows, :]), pick(mine, g_s[rows, :])
            lse = lse_s[rows, head * HEAD_DIM : head * HEAD_DIM + 1]
            scores = masked_tile(dot_nt(q_own, k_s[:reach, :]), diagonal, start)
            probs = jnp.exp(scores - lse)
            grad_probs = dot_nt(g_own, v_s[:reach, :])
            inner = jnp.sum(probs * grad_probs, axis=1, keepdims=True)
            grad_scores = (probs * (grad_probs - inner)).astype(LOW)
            grad_q = jnp.where(mine, dot_nn(grad_scores, k_s[:reach, :]), grad_q)
            dk_s[:reach, :] += dot_tn(grad_scores, q_own)
            dv_s[:reach, :] += dot_tn(probs.astype(LOW), g_own)
        dq_s[rows, :] = grad_q * SCORE_SCALE


def scatter_out_kernel(
    shape, hidden_in, wo_in, g_in, slope_in, qkv_in, lse_in,
    row_in, column_in, start_in, step_in,
    total_out, go_out, gup_out, gm_out,
    hidden_s, wo_s, g_s, slope_s, qkv_s, lse_s, po_s, po_x, po_z, po_sum,
    go_s, go_core, go_y, go_got, gup_s, gctx_s, gm_s, sorted_s, turned_s, dq_s, dk_s, dv_s, sems,
):
    grid = Grid(*shape).locate()
    copies = Copies(sems)
    length, fw = gup_s.shape
    dw = gctx_s.shape[1]
    width, cols = wo_s.shape
    pair = 2 * HEAD_DIM
    loads = [
        copies.local(src, dst)
        for src, dst in (
            (hidden_in, hidden_s), (wo_in, wo_s), (g_in, g_s),
            (slope_in, slope_s), (qkv_in, qkv_s), (lse_in, lse_s),
        )
    ]
    grid.greet()
    loads[0].wait()
    loads[1].wait()
    group = po_s.shape[1]
    tile = min(256, group)
    tokens = TokenScatter(grid, copies, po_s, po_x, po_z, po_sum)
    for t in tokens.order:

        @pl.loop(0, (group // tile) * (width // 256))
        def _(i, t=t):
            part = pl.multiple_of((i // (width // 256)) * tile, tile)
            at = pl.ds(pl.multiple_of((i % (width // 256)) * 256, 256), 256)
            rows = pl.ds(pl.multiple_of(t * group + part, tile), tile)
            result = dot_nt(hidden_s[rows, :], wo_s[at, :])
            po_s[t, pl.ds(part, tile), at] = result.astype(LOW)

        tokens.launch(t)
    loads[2].wait()
    unit = go_s.shape[2]
    block = grid.fsdp_n * unit

    @pl.loop(0, grid.ctx_n)
    def _(c):
        at = pl.ds(pl.multiple_of(c * block, block), block)
        result = dot_tn(g_s[:, at], hidden_s[...]).astype(LOW)
        go_s[c] = result.reshape(grid.fsdp_n, unit, cols)

    shards = ShardScatter(grid, copies, lambda f: [go_s.at[:, f]], go_core, go_y)
    tokens.step(0)
    for k in shards.rounds:
        shards.step(k)
    tokens.step(1)
    loads[3].wait()
    tall = min(256, length)

    @pl.loop(0, (length // tall) * (fw // 256))
    def _(i):
        rows = pl.ds(pl.multiple_of((i // (fw // 256)) * tall, tall), tall)
        at = pl.ds(pl.multiple_of((i % (fw // 256)) * 256, 256), 256)
        grad = dot_nn(g_s[rows, :], wo_s[:, at])
        gup_s[rows, at] = (grad * slope_s[rows, at].astype(F32)).astype(LOW)

    @pl.loop(0, length // tall)
    def _(i):
        rows = pl.ds(pl.multiple_of(i * tall, tall), tall)
        gctx_s[rows, :] = dot_nn(g_s[rows, :], wo_s[:, pl.ds(fw, dw)]).astype(LOW)

    puts = [copies.local(gup_s, gup_out)]
    for i in range(2, grid.z_n):
        tokens.step(i)
    shards.finish()
    peers = [(k, l) for k in range(grid.z_n) for l in range(grid.x_n) if k or l]
    own_o = copies.local(go_s.at[grid.ctx, grid.fsdp], go_got.at[grid.ctx])
    out_sems = [
        copies.send(go_s.at[grid.zx(k, l), grid.fsdp], go_got.at[grid.ctx], ctx=grid.zx(k, l))
        for k, l in peers
    ]
    loads[4].wait()
    loads[5].wait()

    pairs = dw // pair

    @pl.loop(0, length // tall)
    def _(i):
        start = pl.multiple_of(i * tall, tall)
        result = dot_nn(to_sorted(row_in, start, tall), gctx_s[...]).astype(LOW)
        for p in range(pairs):
            sorted_s[p, pl.ds(start, tall), :] = result[:, p * pair : (p + 1) * pair]

    @pl.loop(0, pairs)
    def _(p):
        attend_back(
            qkv_s.at[0, p], qkv_s.at[1, p], qkv_s.at[2, p], lse_s.at[p],
            sorted_s.at[p], dq_s, dk_s, dv_s,
        )

        @pl.loop(0, length // RUN)
        def _(i):
            tables, rows = run_turn(start_in, step_in, i), run_rows(i)
            turned_s[0, p, rows, :] = turn(dq_s[rows, :], tables, -1.0).astype(LOW)
            turned_s[1, p, rows, :] = turn(dk_s[rows, :], tables, -1.0).astype(LOW)
            turned_s[2, p, rows, :] = dv_s[rows, :].astype(LOW)

    @pl.loop(0, length // tall)
    def _(i):
        start = pl.multiple_of(i * tall, tall)
        back = to_stored(column_in, start, tall)
        for kind in range(3):
            for p in range(pairs):
                at = kind * dw + p * pair
                result = dot_nn(back, turned_s[kind, p])
                gm_s[pl.ds(start, tall), at : at + pair] = result.astype(LOW)

    puts.append(copies.local(gm_s, gm_out))
    tokens.finish()
    puts.append(copies.local(po_sum, total_out))
    own_o.wait()
    for (k, l), sem in zip(peers, out_sems):
        arrived(go_got.at[grid.zx(-k, -l)], sem)
    puts.append(copies.local(go_got, go_out))
    for put in puts:
        put.wait()
    copies.drain()


def scatter_in_kernel(
    shape, gm_in, wi_in, gup_in, wu_in, x_in, stats_in, normed_in, g_own_in,
    total_out, gu_out, gi_out, small_out,
    gm_s, wi_s, gup_s, wu_s, x_s, stats_s, normed_s, g_own_s, pn_s, pn_x, pn_z, pn_sum,
    gu_s, gu_core, gu_y, gi_s, gi_core, gi_y, gi_got,
    small_s, small_y, small_x, small_core, small_z, sems,
):
    grid = Grid(*shape).locate()
    copies = Copies(sems)
    length, fw = gup_s.shape
    width = wi_s.shape[1]
    dw = gm_s.shape[1] // 3
    unit = gi_got.shape[1]
    up_rows = fw // grid.fsdp_n
    loads = [
        copies.local(src, dst)
        for src, dst in (
            (gm_in, gm_s), (wi_in, wi_s), (gup_in, gup_s), (wu_in, wu_s),
            (x_in, x_s), (stats_in, stats_s), (normed_in, normed_s), (g_own_in, g_own_s),
        )
    ]
    grid.greet()
    small_s[0] = jnp.zeros_like(small_s[0])
    for load in loads[:6]:
        load.wait()
    group = pn_s.shape[1]
    tile = min(256, group)
    tokens = TokenScatter(grid, copies, pn_s, pn_x, pn_z, pn_sum)
    for t in tokens.order:

        @pl.loop(0, (group // tile) * (width // 256))
        def _(i, t=t):
            part = pl.multiple_of((i // (width // 256)) * tile, tile)
            at = pl.ds(pl.multiple_of((i % (width // 256)) * 256, 256), 256)
            rows = pl.ds(pl.multiple_of(t * group + part, tile), tile)
            grad = dot_nn(gm_s[rows, :], wi_s[:, at]) + dot_nn(gup_s[rows, :], wu_s[:, at])
            pn_s[t, pl.ds(part, tile), at] = grad.astype(LOW)
            mean, spread = stats_s[rows, 0:1], stats_s[rows, HEAD_DIM : HEAD_DIM + 1]
            xhat = (x_s[rows, at].astype(F32) - mean) * spread
            small_s[0, 0:1, at] += jnp.sum(grad * xhat, axis=0, keepdims=True)
            small_s[0, 1:2, at] += jnp.sum(grad, axis=0, keepdims=True)

        tokens.launch(t)
    for load in loads[6:]:
        load.wait()

    small_s[0, 2:3, :] = jnp.sum(g_own_s[...].astype(F32), axis=0, keepdims=True)
    for kind in range(3):
        at = pl.ds(pl.multiple_of(grid.ctx * dw, 128), dw)
        terms = gm_s[:, kind * dw : (kind + 1) * dw].astype(F32)
        small_s[0, 4 + kind : 5 + kind, at] = jnp.sum(terms, axis=0, keepdims=True)
    offset = grid.ctx * fw
    at = pl.ds(pl.multiple_of(offset % width, 128), fw)
    terms = jnp.sum(gup_s[...].astype(F32), axis=0, keepdims=True)
    for row in range(4):
        small_s[0, 7 + row : 8 + row, at] = jnp.where(offset // width == row, terms, 0.0)

    def small_sum(step, buffer, stage):
        for i, sem in enumerate(stage):
            arrived(buffer.at[i], sem)
        accumulate(
            small_s.at[step + 1], small_s.at[step], *[buffer.at[i] for i in range(len(stage))]
        )

    stage = [
        copies.send(small_s.at[0], small_y.at[k - 1], fsdp=grid.yc(k, 0))
        for k in range(1, grid.y_n)
    ]

    @pl.loop(0, 3 * dw // 128)
    def _(i):
        at = pl.ds(pl.multiple_of(i * 128, 128), 128)
        gi_s[at, :] = dot_tn(gm_s[:, at], normed_s[...]).astype(LOW)

    def piece_slot(f, m):
        kind, place = grid.qkv_piece(grid.ctx, f, m)
        return gi_s.at[pl.ds(pl.multiple_of((kind * grid.fsdp_n + place) * unit, unit), unit)]

    shards_i = ShardScatter(
        grid, copies, lambda f: [piece_slot(f, m) for m in range(3)], gi_core, gi_y
    )
    tokens.step(0)
    small_sum(0, small_y, stage)
    stage = [
        copies.send(small_s.at[1], small_core.at[c - 1], fsdp=grid.yc(0, c))
        for c in range(1, grid.core_n)
    ]
    for k in shards_i.rounds:
        shards_i.step(k)

    @pl.loop(0, fw // 128)
    def _(i):
        at = pl.ds(pl.multiple_of(i * 128, 128), 128)
        gu_s[at, :] = dot_tn(gup_s[:, at], normed_s[...]).astype(LOW)

    def up_slot(f):
        return gu_s.at[pl.ds(pl.multiple_of(f * up_rows, up_rows), up_rows)]

    shards_u = ShardScatter(grid, copies, lambda f: [up_slot(f)], gu_core, gu_y)
    tokens.step(1)
    small_sum(1, small_core, stage)
    stage = [
        copies.send(small_s.at[2], small_x.at[l - 1], ctx=grid.zx(0, l))
        for l in range(1, grid.x_n)
    ]
    for k in shards_u.rounds:
        shards_u.step(k)
    tokens.step(2)
    shards_i.finish()
    qkv_sems = []
    for m in range(3):
        owner = grid.qkv_owner(grid.ctx, grid.fsdp, m)
        qkv_sems.append(
            copies.send_or_keep(piece_slot(grid.fsdp, m), gi_got.at[m], owner, grid.ctx)
        )
    for i in range(3, grid.z_n):
        tokens.step(i)
    small_sum(2, small_x, stage)
    stage = [
        copies.send(small_s.at[3], small_z.at[k - 1], ctx=grid.zx(k, 0))
        for k in range(1, grid.z_n)
    ]
    shards_u.finish()
    puts = [copies.local(up_slot(grid.fsdp), gu_out)]
    tokens.finish()
    puts.append(copies.local(pn_sum, total_out))
    for m in range(3):
        arrived(gi_got.at[m], qkv_sems[m])
    puts.append(copies.local(gi_got, gi_out))
    small_sum(3, small_z, stage)
    puts.append(copies.local(small_s.at[4], small_out))
    for put in puts:
        put.wait()
    copies.drain()


def solution(mesh):
    shape = mesh.shape["ctx"], mesh.shape["fsdp"]
    ctx_n, fsdp_n = shape
    n = ctx_n * fsdp_n
    plan = Grid(*shape)
    x_n, z_n, core_n, y_n = plan.x_n, plan.z_n, plan.core_n, plan.y_n

    def gather(x_own, g_own, w_qkv, w_fc1, w_fc2, w_dense, small, tables):
        local_len, width = x_own.shape
        unit, hidden_units = w_fc2.shape
        length = ctx_n * local_len
        fw, dw = hidden_units // ctx_n, width // ctx_n
        pair = 2 * HEAD_DIM
        small_rows = jax.ShapeDtypeStruct((16, width), LOW)
        kept = [
            jax.ShapeDtypeStruct((length, width), LOW),
            jax.ShapeDtypeStruct((length, width), LOW),
            jax.ShapeDtypeStruct((3 * fsdp_n * unit, width), LOW),
            jax.ShapeDtypeStruct((fw, width), LOW),
            jax.ShapeDtypeStruct((ctx_n, fsdp_n, unit, fw + dw), LOW),
        ]
        made = [
            jax.ShapeDtypeStruct((length, width), LOW),
            jax.ShapeDtypeStruct((length, fw + dw), LOW),
            jax.ShapeDtypeStruct((length, fw), LOW),
            jax.ShapeDtypeStruct((3, dw // pair, length, pair), LOW),
            jax.ShapeDtypeStruct((dw // pair, length, pair), F32),
            jax.ShapeDtypeStruct((length, pair), F32),
        ]
        return pl.pallas_call(
            functools.partial(gather_kernel, shape),
            out_shape=kept + [small_rows] + made,
            in_specs=[anywhere] * 6 + [inside] * 5,
            out_specs=[anywhere] * 12,
            scratch_shapes=[pltpu.VMEM(s.shape, s.dtype) for s in kept + made]
            + [pltpu.VMEM((length, 3 * dw), LOW), pltpu.VMEM((dw // pair, length, pair), LOW)]
            + [pltpu.VMEM((16, width), F32), pltpu.VMEM((3, 8, dw), F32)]
            + [pltpu.VMEM((max(fw // 256, 1), 8, min(fw, 256)), F32)]
            + [pltpu.VMEM((count, 16, width), LOW) for count in (5, x_n, core_n, y_n, z_n)]
            + [pltpu.SemaphoreType.DMA((SEMAPHORES,))],
            compiler_params=pltpu.CompilerParams(
                collective_id=0, has_side_effects=True, vmem_limit_bytes=VMEM_BYTES
            ),
            name="gather",
        )(x_own, g_own, w_qkv, w_fc1, w_fc2, w_dense, small, *tables)

    def token_scratch(local_len, width):
        return [
            pltpu.VMEM((z_n, x_n * local_len, width), LOW),
            pltpu.VMEM((z_n, max(x_n - 1, 1), local_len, width), LOW),
            pltpu.VMEM((z_n + 1, local_len, width), LOW),
            pltpu.VMEM((local_len, width), F32),
        ]

    def shard_scratch(parts, *block):
        return [
            pltpu.VMEM((y_n, parts) + block, LOW),
            pltpu.VMEM((max(y_n - 1, 1), parts) + block, LOW),
        ]

    def inside_like(*arrays):
        return [pltpu.VMEM(a.shape, a.dtype) for a in arrays]

    anywhere = pl.BlockSpec(memory_space=pl.ANY)
    inside = pl.BlockSpec(memory_space=pltpu.VMEM)

    def scatter_out(hidden, wo, g_all, slope, qkv, lse, tables):
        length, cols = hidden.shape
        local_len, width = length // ctx_n, g_all.shape[1]
        unit = width // n
        fw = slope.shape[1]
        dw, pair = cols - fw, 2 * HEAD_DIM
        return pl.pallas_call(
            functools.partial(scatter_out_kernel, shape),
            out_shape=[
                jax.ShapeDtypeStruct((local_len, width), F32),
                jax.ShapeDtypeStruct((ctx_n, unit, cols), LOW),
                jax.ShapeDtypeStruct((length, fw), LOW),
                jax.ShapeDtypeStruct((length, 3 * dw), LOW),
            ],
            in_specs=[anywhere] * 6 + [inside] * 4,
            out_specs=[anywhere] * 4,
            scratch_shapes=inside_like(hidden, wo, g_all, slope, qkv, lse)
            + token_scratch(local_len, width)
            + [pltpu.VMEM((ctx_n, fsdp_n, unit, cols), LOW)]
            + shard_scratch(1, ctx_n, unit, cols)
            + [pltpu.VMEM((ctx_n, unit, cols), LOW)]
            + [pltpu.VMEM((length, c), LOW) for c in (fw, dw, 3 * dw)]
            + [pltpu.VMEM((dw // pair, length, pair), LOW)]
            + inside_like(qkv)
            + [pltpu.VMEM((length, pair), F32)] * 3
            + [pltpu.SemaphoreType.DMA((SEMAPHORES,))],
            compiler_params=pltpu.CompilerParams(
                collective_id=1, has_side_effects=True, vmem_limit_bytes=VMEM_BYTES
            ),
            name="scatter_out",
        )(hidden, wo, g_all, slope, qkv, lse, *tables)

    def scatter_in(gm, wi, gup, wu, x_all, stats, normed, g_own):
        length, width = normed.shape
        local_len = length // ctx_n
        unit, up_rows = width // n, wu.shape[0] // fsdp_n
        return pl.pallas_call(
            functools.partial(scatter_in_kernel, shape),
            out_shape=[
                jax.ShapeDtypeStruct((local_len, width), F32),
                jax.ShapeDtypeStruct((up_rows, width), LOW),
                jax.ShapeDtypeStruct((3, unit, width), LOW),
                jax.ShapeDtypeStruct((16, width), F32),
            ],
            in_specs=[anywhere] * 8,
            out_specs=[anywhere] * 4,
            scratch_shapes=inside_like(gm, wi, gup, wu, x_all, stats, normed, g_own)
            + token_scratch(local_len, width)
            + inside_like(wu)
            + shard_scratch(1, up_rows, width)
            + inside_like(wi)
            + shard_scratch(3, unit, width)
            + [pltpu.VMEM((3, unit, width), LOW)]
            + [pltpu.VMEM((count, 16, width), F32) for count in (5, y_n, x_n, core_n, z_n)]
            + [pltpu.SemaphoreType.DMA((SEMAPHORES,))],
            compiler_params=pltpu.CompilerParams(
                collective_id=2, has_side_effects=True, vmem_limit_bytes=VMEM_BYTES
            ),
            name="scatter_in",
        )(gm, wi, gup, wu, x_all, stats, normed, g_own)

    def body(
        hidden_in, positions, ln_gain, ln_bias, w_qkv, b_qkv, w_dense, b_dense,
        w_fc1, b_fc1, w_fc2, b_fc2, out_grad,
    ):
        local_len, width = hidden_in.shape[1:]
        hidden_units = w_fc2.shape[1]
        unit = w_dense.shape[0]
        up_rows = w_fc1.shape[0]
        fw, dw = hidden_units // ctx_n, width // ctx_n
        my_ctx = lax.axis_index("ctx")
        me = my_ctx * fsdp_n + lax.axis_index("fsdp")
        length = positions.shape[1]
        x_own, g_own = hidden_in[0], out_grad[0]

        rank = positions[0, ::RUN] // RUN
        starts, steps = turning_tables(length)
        ranks = jnp.arange(length // RUN, dtype=jnp.int32)
        chosen = (rank[:, None] == ranks[None, :])[None, :, :, None]
        stored_starts = jnp.sum(jnp.where(chosen, starts[:, None], 0.0), axis=2)
        places = positions, positions.reshape(length, 1)

        own_small = jnp.concatenate([ln_gain, ln_bias, b_dense, b_fc2, b_qkv, b_fc1])
        own_small = jnp.pad(own_small.reshape(-1, unit), ((0, 5), (0, width - unit)))
        x_all, g_all, wi, wu, wo, small, normed, hidden, slope, qkv, lse, stats = gather(
            x_own, g_own, w_qkv, w_fc1, w_fc2, w_dense, own_small, (*places, stored_starts, steps)
        )
        small = small.astype(F32)
        gain, bias_dense, bias_down = small[0], small[2], small[3]
        total, grad_o, grad_upward, grad_mixed = scatter_out(
            hidden, wo.reshape(width, fw + dw), g_all, slope, qkv, lse, (*places, starts, steps)
        )
        grad_normed, grad_up, grad_qkv, sums = scatter_in(
            grad_mixed, wi, grad_upward, wu, x_all, stats, normed, g_own
        )

        def standardize(values):
            wide = values.astype(F32)
            centered = wide - jnp.mean(wide, axis=-1, keepdims=True)
            spread = lax.rsqrt(jnp.mean(centered * centered, axis=-1, keepdims=True) + EPSILON)
            return centered * spread, spread

        hidden_out = (total + x_own.astype(F32) + bias_dense + bias_down).astype(LOW)
        xhat, spread = standardize(x_own)
        e = grad_normed * gain
        grad_in = (
            e - jnp.mean(e, axis=-1, keepdims=True)
            - xhat * jnp.mean(e * xhat, axis=-1, keepdims=True)
        ) * spread + g_own.astype(F32)
        grad_o = grad_o.transpose(1, 0, 2).astype(F32)
        sums = sums.reshape(-1)

        def own_slice(row, size):
            return lax.dynamic_slice_in_dim(sums, row * width + me * size, size)

        grad_b_out = own_slice(2, unit)
        return (
            hidden_out[None],
            grad_in[None],
            own_slice(0, unit),
            own_slice(1, unit),
            grad_qkv.reshape(3 * unit, width).astype(F32),
            own_slice(4, 3 * unit),
            grad_o[:, :, fw:].reshape(unit, width),
            grad_b_out,
            grad_up.astype(F32),
            own_slice(7, up_rows),
            grad_o[:, :, :fw].reshape(unit, hidden_units),
            grad_b_out,
        )

    tokens, rows, cells = P("fsdp", "ctx", None), P(BOTH, None), P(BOTH)
    return jax.shard_map(
        body,
        mesh=mesh,
        in_specs=(
            tokens, P("fsdp", None), cells, cells, rows, cells, rows, cells,
            rows, cells, rows, cells, tokens,
        ),
        out_specs=(
            tokens, tokens, cells, cells, rows, cells, rows, cells, rows, cells, rows, cells,
        ),
        check_vma=False,
    )
```

time: 439 us -> 398 us (0.907)
  the two profiles are of different devices: /device:TPU:6 before, /device:TPU:10 now
where the time goes in v2:
time: 398 us; the launch traced here: 392 us
  Pallas kernels  370 us (93%)
  local copies, waits for them, and re-layouts  13.3 us (3%)
  other arithmetic  8.73 us (2%)
    pallas_call x1, Pallas kernels, gather(): pl.pallas_call(functools.partial(gather_kernel, shape), out_shape=kept +...  152 us
    pallas_call x1, Pallas kernels, scatter_out(): pl.pallas_call(functools.partial(scatter_out_kernel, shape), out_shape=[j...  109 us
    pallas_call x1, Pallas kernels, scatter_in(): pl.pallas_call(functools.partial(scatter_in_kernel, shape), out_shape=[ja...  108 us

profile of v2, /device:TPU:10, one launch (start us, length us, event | category | flops | bytes accessed | tf_op | source)
XLA Modules:
  0.0 392.4 jit_solution(10471525648712894753)
XLA Ops:
  0.6 1.7 copy.32.column_in
  2.4 4.1 %concatenate.3 = bf16[704]{0:T(1024)(128)(2,1)S(1)} concatenate(bf16[64]{0:T(256)(128)(2,1)} %param.18, bf16[64]{0:T(256)(128)(2,1)} %param.19, bf16[64]{0:T(256)(128)(2,1)} %param.23, bf16[64]{0:T(256)(128)(2,1)} %param.27, bf16[192]{0:T(256)(128)(2,1)} %param.21, bf16[256]{0:T(256)(128)(2,1)} %param.25), dimensions={0} | concatenate | bytes 2816 | tf_op jit(solution)/shard_map/concatenate | solution.py:1216
  6.4 0.1 reshape.115
  6.5 0.6 pad.4.small_in
  7.2 0.8 slice.18
  8.0 0.1 iota_compare_fusion
  8.0 1.5 select_reduce_fusion.start_in
  9.5 152.3 %gather.1 = (bf16[1024,2048]{1,0:T(8,128)(2,1)}, bf16[1024,2048]{1,0:T(8,128)(2,1)}, bf16[768,2048]{1,0:T(8,128)(2,1)}, bf16[1024,2048]{1,0:T(8,128)(2,1)}, bf16...) custom-call(bf16[128,2048]{1,0:T(8,128)(2,1)} %bitcast.38, ...), custom_call_target="tpu_custom_call" | custom-call | tf_op jit(solution)/shard_map/gather/pallas_call | solution.py:1097
  161.8 109.2 %scatter_out.1 = (f32[128,2048]{1,0:T(8,128)}, bf16[8,64,1280]{2,1,0:T(8,128)(2,1)}, bf16[1024,1024]{1,0:T(8,128)(2,1)}, bf16[1024,768]{1,0:T(8,128)(2,1)}) custom-call(bf16[1024,1280]{1,0:T(8,128)(2,1)} %get-tuple-element.32.hidden_in, bf16[2048,1280]{1,0:T(8,128)(2,1)} %bitcast.39, bf16[1024,2048]{1,0:T(8,128)(2,1)} %get-tuple-element.34.g_in, ...), custom_call_target="tpu_custom_call" | custom-call | tf_op jit(solution)/shard_map/scatter_out/pallas_call | solution.py:1140
  271.0 108.1 %scatter_in.1 = (f32[128,2048]{1,0:T(8,128)}, bf16[256,2048]{1,0:T(8,128)(2,1)}, bf16[3,64,2048]{2,1,0:T(8,128)(2,1)}, f32[16,2048]{1,0:T(8,128)}) custom-call(bf16[1024,768]{1,0:T(8,128)(2,1)} %get-tuple-element.40.gm_in, bf16[768,2048]{1,0:T(8,128)(2,1)} %get-tuple-element.41.wi_in, bf16[1024,1024]{1,0:T(8,128)(2,1)} %get-tuple-element.42.gup_in, ...), custom_call_target="tpu_custom_call" | custom-call | tf_op jit(solution)/shard_map/scatter_in/pallas_call | solution.py:1170
  379.2 0.0 copy-start
  379.2 0.0 copy-start.2
  379.2 2.9 convert_element_type.38
  382.1 0.0 copy-start.1
  382.1 0.0 copy-start.4
  382.1 0.9 fusion.15
  383.0 0.0 copy-done
  383.0 0.2 convert_reduce_fusion
  383.2 0.3 fusion.9
  383.5 0.0 copy-done.2
  383.5 0.4 multiply_reduce_fusion
  383.9 0.0 copy-done.1
  383.9 0.0 copy-done.4
  383.9 0.0 copy-start.5
  383.9 1.8 fusion.8
  385.7 0.0 copy-start.6
  385.7 0.0 copy-start.3
  385.7 0.0 copy-done.5
  385.7 1.4 bitcast_convert_fusion
  387.1 0.0 copy-done.6
  387.2 0.6 fusion.14
  387.8 0.0 copy-start.7
  387.8 0.6 dynamic_slice.17
  388.4 0.6 dynamic_slice.19
  389.0 0.0 copy-done.3
  389.0 0.2 convert_bitcast_fusion
  389.3 0.3 slice_bitcast_fusion
  389.6 1.5 copy.37
  391.1 0.8 copy.36
  391.9 0.0 copy-done.7
  391.9 0.5 copy.40
  (6 shorter events, 0.1 us)
Async XLA Ops:
  379.2 3.9 copy-start
  379.2 4.3 %copy-start.2 = (f32[128,2048]{1,0:T(8,128)S(1)}, f32[128,2048]{1,0:T(8,128)}, u32[]{:S(2)}) copy-start(f32[128,2048]{1,0:T(8,128)} %get-tuple-element.47) | copy-start | bytes 3145732
  382.1 1.8 copy-start.1
  382.1 1.8 copy-start.4
  383.9 1.9 copy-start.5
  385.7 1.4 copy-start.6
  385.7 3.3 copy-start.3
  387.8 4.2 %copy-start.7 = (f32[64]{0:T(128)}, f32[64]{0:T(128)S(1)}, u32[]{:S(2)}) copy-start(f32[64]{0:T(128)S(1)} %get-tuple-element.87) | copy-start | bytes 772
